TPU v7x, 32 devices: a whole 2x2x4 slice. The times are simulated.
32 devices in a mesh: qx: 8 (over z, y), qy: 4 (over x, core).
Axes of the slice: x: 2, y: 2, z: 4, core: 2. Of those that a mesh axis runs over, the one named last changes fastest.
Arguments:
- vectors: bfloat16 [64, 256, 512], P(None, 'qx', 'qy'), may hold values from -6 to 6
- near_tiles: bfloat16 [16, 32, 3, 256, 256], P('qx', 'qy'), may hold values from -0.21875 to 0.21875
- near_offset: int32 [16, 32, 3], P('qx', 'qy'), may hold values from 0 to 8, as said below
- col_basis: bfloat16 [16, 32, 64, 256], P('qx', 'qy'), may hold values from -0.375 to 0.375
- row_basis: bfloat16 [16, 32, 64, 256], P('qx', 'qy'), may hold values from -0.375 to 0.375
- up_transfer: float32 [16, 32, 64, 64], P('qx', 'qy'), may hold values from -0.375 to 0.375
- down_transfer: float32 [16, 32, 64, 64], P('qx', 'qy'), may hold values from -0.75 to 0.75
- coupling: float32 [32, 128, 64, 64], P(('qx', 'qy')), may hold values from -0.75 to 0.75
- couple_dest: int32 [32, 128], replicated, may hold values from -1 to 31, as said below
- couple_target: int32 [32, 128], replicated, may hold values from 0 to 19, as said below
Outputs:
- product: float32 [64, 256, 512], P(None, 'qx', 'qy')
Inputs may be any that keep to these rules, and one draw needn't show every extreme that they name: `couple_dest`: in each row (source device) no destination device appears more than 4 times; in every draw one destination device appears exactly 4 times in every row; -1 marks a padded slot. `couple_target`: slots below 96 name a leaf cluster (0 to 15), the others a parent cluster (16 to 19) of the target device. `near_offset`: the 3 codes of a leaf are distinct; code o reads the leaf at offset (o // 3 - 1, o % 3 - 1).
All inputs are finite; a program needn't handle non-finite values.
Results may differ from a plain program's by a relative error of at most 0.0003.
Values may be sent and summed in bfloat16 or wider, within the bound.
A program may use at most 64 MiB of HBM per device.

v0:
```python
import jax
import jax.numpy as jnp
from jax import lax
from jax.sharding import PartitionSpec as P

LS = 16
K0 = 6
K1 = 8


def extended(array, sides, width):
    for axis, dim in sides:
        peers, length = (lax.axis_size(axis), array.shape[dim])
        up = [(i, (i + 1) % peers) for i in range(peers - 1)]
        down = [(j, i) for i, j in up]
        last = lax.slice_in_dim(array, length - width, length, axis=dim)
        initial = lax.slice_in_dim(array, 0, width, axis=dim)
        before = lax.ppermute(last, axis, up)
        after = lax.ppermute(initial, axis, down)
        array = jnp.concatenate([before, array, after], axis=dim)
    return array


def arrival_map(dest_rows, target_rows, wanted, capacity, cluster_count):
    matches = dest_rows == wanted
    counts = matches.astype(jnp.int32)
    order_in = jnp.cumsum(counts, axis=-1) - counts
    landing = (
        matches[..., None] & (order_in[..., None] == jnp.arange(capacity, dtype=jnp.int32))
    ).astype(jnp.float32)
    chosen = (
        jnp.broadcast_to(target_rows, matches.shape)[..., None]
        == jnp.arange(cluster_count, dtype=jnp.int32)
    ).astype(jnp.float32)
    return jnp.einsum("...sc,...sn->...cn", landing, chosen, precision=lax.Precision.HIGHEST)


def body(
    vectors,
    near_tiles,
    near_offset,
    col_basis,
    row_basis,
    up_transfer,
    down_transfer,
    coupling,
    couple_dest,
    couple_target,
):
    precise = lax.Precision.HIGHEST
    width_x = lax.axis_size("qx")
    width_y = lax.axis_size("qy")
    devices = width_x * width_y
    vec_count, rows_x, rows_y = vectors.shape
    leaf_x = rows_x // LS
    leaf_y = rows_y // LS
    leaf_count = leaf_x * leaf_y
    upper_count = leaf_y // 2
    cluster_count = leaf_count + upper_count
    rank_size = coupling.shape[2]
    slot_count = coupling.shape[1]
    capacity = (slot_count + devices - 1) // devices
    points = LS * LS
    flat_size = rank_size * vec_count
    my_index = lax.axis_index("qx") * width_y + lax.axis_index("qy")
    blocks = (
        vectors.reshape(vec_count, leaf_x, LS, leaf_y, LS)
        .transpose(1, 3, 0, 2, 4)
        .reshape(leaf_x, leaf_y, vec_count, points)
    )
    leaf_coef = jnp.einsum("ijrp,ijvp->ijrv", col_basis, blocks, preferred_element_type=jnp.float32)
    lifted = jnp.einsum("ijrs,ijsv->ijrv", up_transfer, leaf_coef, precision=precise)
    upper_coef = lifted.reshape(leaf_x, upper_count, 2, rank_size, vec_count).sum(axis=(0, 2))
    sources = jnp.concatenate(
        [
            jnp.repeat(leaf_coef.reshape(leaf_count, rank_size, vec_count), K0, axis=0),
            jnp.repeat(upper_coef, K1, axis=0),
        ],
        axis=0,
    )
    contrib = jnp.einsum("srt,stv->srv", coupling[0], sources, precision=precise).reshape(
        slot_count, flat_size
    )
    own_dest = lax.dynamic_index_in_dim(couple_dest, my_index, 0, keepdims=False)
    slot_ident = jnp.arange(slot_count, dtype=jnp.int32)
    same_dest = own_dest[:, None] == own_dest[None, :]
    earlier = slot_ident[:, None] > slot_ident[None, :]
    order_in = jnp.sum((same_dest & earlier).astype(jnp.int32), axis=1)
    spare_row = devices * capacity
    position = jnp.where(own_dest >= 0, own_dest * capacity + order_in, spare_row)
    placed = jnp.zeros((spare_row + 1, flat_size), jnp.float32).at[position].set(contrib)
    outgoing = placed[:spare_row].reshape(width_x, width_y, capacity, flat_size)
    first_hop = lax.all_to_all(outgoing, "qx", split_axis=0, concat_axis=0, tiled=True)
    dest_rows = lax.dynamic_index_in_dim(
        couple_dest.reshape(width_x, width_y, slot_count), lax.axis_index("qy"), 1, keepdims=False
    )
    target_rows = lax.dynamic_index_in_dim(
        couple_target.reshape(width_x, width_y, slot_count), lax.axis_index("qy"), 1, keepdims=False
    )
    wanted = lax.axis_index("qx") * width_y + jnp.arange(width_y, dtype=jnp.int32)
    arrival = arrival_map(
        dest_rows[:, None, :],
        target_rows[:, None, :],
        wanted[None, :, None],
        capacity,
        cluster_count,
    )
    partial_value = jnp.einsum("ajcn,ajcf->jnf", arrival, first_hop, precision=precise)
    second = lax.all_to_all(partial_value, "qy", split_axis=0, concat_axis=0, tiled=True)
    far_coef = jnp.sum(second, axis=0)
    far_coef = far_coef.reshape(cluster_count, rank_size, vec_count)
    down_leaf = far_coef[:leaf_count].reshape(leaf_x, leaf_y, rank_size, vec_count)
    expanded = jnp.broadcast_to(
        jnp.repeat(far_coef[leaf_count:], 2, axis=0)[None], (leaf_x, leaf_y, rank_size, vec_count)
    )
    down_leaf = down_leaf + jnp.einsum(
        "ijrs,ijsv->ijrv", down_transfer, expanded, precision=precise
    )
    far_out = jnp.einsum(
        "ijrp,ijrv->ijvp", row_basis.astype(jnp.float32), down_leaf, precision=precise
    )
    padded = extended(vectors, (("qx", 1), ("qy", 2)), LS)
    padded_blocks = (
        padded.reshape(vec_count, leaf_x + 2, LS, leaf_y + 2, LS)
        .transpose(1, 3, 0, 2, 4)
        .reshape((leaf_x + 2) * (leaf_y + 2), vec_count, points)
    )
    along_x = jnp.arange(leaf_x, dtype=jnp.int32)[:, None, None]
    along_y = jnp.arange(leaf_y, dtype=jnp.int32)[None, :, None]
    tile_index = (along_x + near_offset // 3) * (leaf_y + 2) + along_y + near_offset % 3
    picked = padded_blocks[tile_index]
    near_out = jnp.einsum(
        "ijkps,ijkvs->ijvp", near_tiles, picked, preferred_element_type=jnp.float32
    )
    total_out = near_out + far_out
    return (
        total_out.reshape(leaf_x, leaf_y, vec_count, LS, LS)
        .transpose(2, 0, 3, 1, 4)
        .reshape(vec_count, rows_x, rows_y)
    )


def solution(mesh):
    return jax.shard_map(
        body,
        mesh=mesh,
        in_specs=(
            P(None, "qx", "qy"),
            P("qx", "qy", None, None, None),
            P("qx", "qy", None),
            P("qx", "qy", None, None),
            P("qx", "qy", None, None),
            P("qx", "qy", None, None),
            P("qx", "qy", None, None),
            P(("qx", "qy"), None, None, None),
            P(),
            P(),
        ),
        out_specs=P(None, "qx", "qy"),
        check_vma=False,
    )
```

profile of v0, /device:TPU:16, one launch (start us, length us, event | category | flops | bytes accessed | tf_op | source)
XLA Modules:
  0.0 150.7 jit_solution(9276007782464418942)
XLA Ops:
  1.7 1.8 %copy.85 = bf16[64,32,128]{0,2,1:T(8,128)(2,1)S(1)} copy(bf16[64,32,128]{2,1,0:T(8,128)(2,1)} %param.10) | data formatting | bytes 1048576 | tf_op args[0]
  5.3 5.6 %copy.98 = f32[128,64,64]{2,1,0:T(8,128)} copy(f32[128,64,64]{0,2,1:T(8,128)} %bitcast.83) | data formatting | bytes 4194304 | tf_op jit(solution)/shard_map/squeeze | solution.py:81
  11.4 1.7 %copy-done.1 = f32[128,64,64]{2,1,0:T(8,128)S(1)} copy-done((f32[128,64,64]{2,1,0:T(8,128)S(1)}, f32[128,64,64]{2,1,0:T(8,128)}, u32[]{:S(2)}) %copy-start.1) | copy-done | bytes 2097176
  13.1 8.8 %fusion.4 = f32[128,64,64]{1,2,0:T(8,128)} fusion(f32[128,64,64]{2,1,0:T(8,128)S(1)} %copy-done.1, f32[32,64,64]{1,2,0:T(8,128)S(1)} %bitcast.81, f32[96,64,64]{1,2,0:T(8,128)S(1)} %bitcast.73), kind=kOutput, calls=%fused_computation.8 | convolution fusion | flops 403177472 | bytes 6291456 | tf_op jit(solution)/shard_map/srt,stv->srv/dot_general | solution.py:81
  21.9 5.3 %copy.99 = f32[128,64,64]{0,2,1:T(8,128)} copy(f32[128,64,64]{1,2,0:T(8,128)} %fusion.4) | data formatting | bytes 4194304 | tf_op jit(solution)/shard_map/srt,stv->srv/dot_general | solution.py:81
  27.3 2.9 %copy.100 = f32[128,4096]{1,0:T(8,128)} copy(f32[128,4096]{0,1:T(8,128)} %bitcast.75) | data formatting | bytes 4194304 | tf_op jit(solution)/shard_map/reshape | solution.py:81
  30.2 4.3 %scatter_custom_fusion = f32[129,4096]{1,0:T(8,128)} fusion(s32[128]{0:T(128)S(1)} %fusion.19, f32[128,4096]{1,0:T(8,128)} %copy.100, f32[]{:T(128)} %constant.56.clone.1), kind=kCustom, calls=%fused_computation.13 | custom fusion | bytes 2114048 | tf_op jit(solution)/shard_map/scatter | solution.py:91
  34.5 3.1 %slice.37 = f32[128,4096]{1,0:T(8,128)} slice(f32[129,4096]{1,0:T(8,128)} %scatter_custom_fusion), slice={[0:128], [0:4096]} | slice | bytes 4194304 | tf_op jit(solution)/shard_map/slice | solution.py:92
  37.6 2.8 %reshape.118 = f32[8,4,4,4096]{3,2,1,0:T(4,128)} reshape(f32[128,4096]{1,0:T(8,128)} %slice.37) | data formatting | bytes 4194304 | tf_op jit(solution)/shard_map/reshape | solution.py:92
  40.4 6.3 %all-to-all-start = ((f32[8,4,4,4096]{3,2,1,0:T(4,128)}), f32[8,4,4,4096]{3,2,1,0:T(4,128)}, u32[]{:S(2)}, u32[]{:S(2)}) async-start(f32[8,4,4,4096]{3,2,1,0:T(4,128)} %reshape.118), calls=%async_computation | async-start | bytes 4194304 | tf_op jit(solution)/shard_map/all_to_all | solution.py:93
  47.6 3.4 %collective-permute-start = (bf16[64,16,128]{0,2,1:T(8,128)(2,1)}, bf16[64,16,128]{0,2,1:T(8,128)(2,1)S(1)}, u32[]{:S(2)}, u32[]{:S(2)}) collective-permute-start(bf16[64,16,128]{0,2,1:T(8,128)(2,1)} %get-tuple-element.9), channel_id=1, source_target_pairs={{0,4},{4,8},{8,12},{12,16},{16,20},{20,24},{24,28},{1,5},{5,9},{9,... | collective-permute-start | bytes 786440 | tf_op jit(solution)/shard_map/ppermute | solution.py:18
  51.0 3.6 %collective-permute-start.1 = (bf16[64,16,128]{0,2,1:T(8,128)(2,1)S(1)}, bf16[64,16,128]{0,2,1:T(8,128)(2,1)S(1)}, u32[]{:S(2)}, u32[]{:S(2)}) collective-permute-start(bf16[64,16,128]{0,2,1:T(8,128)(2,1)S(1)} %get-tuple-element.10), channel_id=1, source_target_pairs={{4,0},{8,4},{12,8},{16,12},{20,16},{24,20},{28,24},{5,1},{9,5},{13... | collective-permute-start | bytes 786440 | tf_op jit(solution)/shard_map/ppermute | solution.py:19
  57.0 47.8 %collective-permute-done = bf16[64,16,128]{0,2,1:T(8,128)(2,1)S(1)} collective-permute-done((bf16[64,16,128]{0,2,1:T(8,128)(2,1)}, bf16[64,16,128]{0,2,1:T(8,128)(2,1)S(1)}, u32[]{:S(2)}, u32[]{:S(2)}) %collective-permute-start) | collective-permute-done | bytes 262176 | tf_op jit(solution)/shard_map/ppermute | solution.py:18
  105.8 1.9 %collective-permute-start.2 = (bf16[64,64,16]{0,2,1:T(8,128)(2,1)}, bf16[64,64,16]{0,2,1:T(8,128)(2,1)S(1)}, u32[]{:S(2)}, u32[]{:S(2)}) collective-permute-start(bf16[64,64,16]{0,2,1:T(8,128)(2,1)} %get-tuple-element.7), channel_id=1, source_target_pairs={{0,1},{1,2},{2,3},{4,5},{5,6},{6,7},{8,9},{9,10},{10,11},{12,13},{... | collective-permute-start | bytes 393224 | tf_op jit(solution)/shard_map/ppermute | solution.py:18
  109.1 5.3 %convolution_bitcast_fusion = f32[4,20,4096]{2,1,0:T(8,128)} fusion(f32[8,4,4,20]{3,2,1,0:T(4,128)S(1)} %fusion.10, f32[8,4,4,4096]{3,2,1,0:T(4,128)} %all-to-all-done), kind=kOutput, calls=%fused_computation.2 | convolution fusion | flops 125829120 | bytes 3418112 | tf_op jit(solution)/shard_map/ajcn,ajcf->jnf/dot_general | solution.py:108
  114.3 5.1 %all-to-all-start.1 = ((f32[4,20,4096]{2,1,0:T(8,128)}), f32[4,20,4096]{2,1,0:T(8,128)S(1)}, u32[]{:S(2)}, u32[]{:S(2)}) async-start(f32[4,20,4096]{2,1,0:T(8,128)} %convolution_bitcast_fusion), calls=%async_computation.1 | async-start | bytes 3145728 | tf_op jit(solution)/shard_map/all_to_all | solution.py:109
  119.4 2.8 %pad_maximum_fusion = bf16[64,64,160]{0,2,1:T(8,128)(2,1)S(1)} fusion(bf16[64,64,16]{0,2,1:T(8,128)(2,1)} %collective-permute-done.3, bf16[64,16,128]{0,2,1:T(8,128)(2,1)} %copy-done.3, bf16[64,32,128]{0,2,1:T(8,128)(2,1)S(1)} %copy.85, bf16[64,16,128]{0,2,1:T(8,128)(2,1)} %copy-done.2, bf16[64,64,16]{0,2,1:T(8,128)(2,1)S(1)} %collective-permute-done.2), kind=kLoop, calls=%fused_computation.7 | loop fusion | flops 6553600 | bytes 2621440 | tf_op jit(solution)/shard_map/concatenate | solution.py:20
  122.3 2.3 %copy.88 = bf16[4,10,64,16,16]{2,4,3,1,0:T(8,128)(2,1)} copy(bf16[4,10,64,16,16]{2,4,1,3,0:T(8,128)(2,1)S(1)} %bitcast.74) | data formatting | bytes 2621440 | tf_op jit(solution)/shard_map/transpose | solution.py:125
  124.6 4.4 %gather_fusion = bf16[48,64,256]{1,2,0:T(8,128)(2,1)} fusion(bf16[40,64,256]{1,2,0:T(8,128)(2,1)} %bitcast.79, s32[1024]{0:T(1024)S(1)} %pad_clamp_fusion), kind=kCustom, calls=%fused_computation | custom fusion | bytes 3145920 | tf_op jit(solution)/shard_map/gather | solution.py:131
  129.0 5.8 %convolution_bitcast_fusion.1 = f32[2,8,64,256]{3,2,1,0:T(8,128)S(1)} fusion(bf16[2,8,3,64,256]{3,4,2,1,0:T(8,128)(2,1)} %bitcast.78, bf16[2,8,3,256,256]{4,3,2,1,0:T(8,128)(2,1)} %param.11), kind=kOutput, calls=%fused_computation.10 | convolution fusion | flops 402653184 | bytes 8912896 | tf_op jit(solution)/shard_map/ijkps,ijkvs->ijvp/dot_general | solution.py:132
  134.8 4.7 %all-to-all-done.1 = f32[4,20,4096]{2,1,0:T(8,128)S(1)} async-done(((f32[4,20,4096]{2,1,0:T(8,128)}), f32[4,20,4096]{2,1,0:T(8,128)S(1)}, u32[]{:S(2)}, u32[]{:S(2)}) %all-to-all-start.1) | async-done | bytes 1310752 | tf_op jit(solution)/shard_map/all_to_all | solution.py:109
  142.2 2.0 %copy.103 = f32[2,8,64,256]{2,3,1,0:T(8,128)} copy(f32[2,8,64,256]{3,2,1,0:T(8,128)S(1)} %convolution_add_fusion) | data formatting | bytes 2097152 | tf_op jit(solution)/shard_map/add | solution.py:135
  144.1 3.2 %copy.104 = f32[64,2,16,8,16]{0,4,3,2,1:T(8,128)} copy(f32[64,2,16,8,16]{0,4,2,3,1:T(8,128)} %bitcast.76) | data formatting | bytes 2097152 | tf_op jit(solution)/shard_map/transpose | solution.py:138
  147.3 3.4 %copy.105 = f32[64,32,128]{2,1,0:T(8,128)} copy(f32[64,32,128]{0,2,1:T(8,128)} %bitcast.77) | data formatting | bytes 2097152 | tf_op jit(solution)/shard_map/reshape | solution.py:139
  (54 shorter events, 12.2 us)
Async XLA Ops:
  0.0 141.6 %copy-start = (bf16[2,8,64,256]{3,2,1,0:T(8,128)(2,1)S(1)}, bf16[2,8,64,256]{3,2,1,0:T(8,128)(2,1)}, u32[]{:S(2)}) copy-start(bf16[2,8,64,256]{3,2,1,0:T(8,128)(2,1)} %param.14) | copy-start | bytes 1572868
  0.0 3.7 %copy-start.6 = (bf16[2,8,64,256]{3,2,1,0:T(8,128)(2,1)S(1)}, bf16[2,8,64,256]{3,2,1,0:T(8,128)(2,1)}, u32[]{:S(2)}) copy-start(bf16[2,8,64,256]{3,2,1,0:T(8,128)(2,1)} %param.13) | copy-start | bytes 1572868
  1.7 2.4 %copy-start.5 = (f32[2,8,64,64]{3,2,1,0:T(8,128)S(1)}, f32[2,8,64,64]{3,2,1,0:T(8,128)}, u32[]{:S(2)}) copy-start(f32[2,8,64,64]{3,2,1,0:T(8,128)} %param.15) | copy-start | bytes 786436
  10.9 2.2 %copy-start.1 = (f32[128,64,64]{2,1,0:T(8,128)S(1)}, f32[128,64,64]{2,1,0:T(8,128)}, u32[]{:S(2)}) copy-start(f32[128,64,64]{2,1,0:T(8,128)} %copy.98) | copy-start | bytes 6291460
  40.4 16.1 %copy-start.7 = (s32[2,8,3]{1,0,2:T(2,128)S(1)}, s32[2,8,3]{1,0,2:T(2,128)}, u32[]{:S(2)}) copy-start(s32[2,8,3]{1,0,2:T(2,128)} %param.12) | copy-start | bytes 580
  40.4 68.6 %all-to-all-start = ((f32[8,4,4,4096]{3,2,1,0:T(4,128)}), f32[8,4,4,4096]{3,2,1,0:T(4,128)}, u32[]{:S(2)}, u32[]{:S(2)}) async-start(f32[8,4,4,4096]{3,2,1,0:T(4,128)} %reshape.118), calls=%async_computation | async-start | bytes 4194304 | tf_op jit(solution)/shard_map/all_to_all | solution.py:93
  47.6 57.2 %collective-permute-start = (bf16[64,16,128]{0,2,1:T(8,128)(2,1)}, bf16[64,16,128]{0,2,1:T(8,128)(2,1)S(1)}, u32[]{:S(2)}, u32[]{:S(2)}) collective-permute-start(bf16[64,16,128]{0,2,1:T(8,128)(2,1)} %get-tuple-element.9), channel_id=1, source_target_pairs={{0,4},{4,8},{8,12},{12,16},{16,20},{20,24},{24,28},{1,5},{5,9},{9,... | collective-permute-start | bytes 786440 | tf_op jit(solution)/shard_map/ppermute | solution.py:18
  51.0 53.8 %collective-permute-start.1 = (bf16[64,16,128]{0,2,1:T(8,128)(2,1)S(1)}, bf16[64,16,128]{0,2,1:T(8,128)(2,1)S(1)}, u32[]{:S(2)}, u32[]{:S(2)}) collective-permute-start(bf16[64,16,128]{0,2,1:T(8,128)(2,1)S(1)} %get-tuple-element.10), channel_id=1, source_target_pairs={{4,0},{8,4},{12,8},{16,12},{20,16},{24,20},{28,24},{5,1},{9,5},{13... | collective-permute-start | bytes 786440 | tf_op jit(solution)/shard_map/ppermute | solution.py:19
  104.8 9.5 %copy-start.2 = (bf16[64,16,128]{0,2,1:T(8,128)(2,1)}, bf16[64,16,128]{0,2,1:T(8,128)(2,1)S(1)}, u32[]{:S(2)}) copy-start(bf16[64,16,128]{0,2,1:T(8,128)(2,1)S(1)} %collective-permute-done) | copy-start | bytes 786436
  104.8 9.5 %copy-start.3 = (bf16[64,16,128]{0,2,1:T(8,128)(2,1)}, bf16[64,16,128]{0,2,1:T(8,128)(2,1)S(1)}, u32[]{:S(2)}) copy-start(bf16[64,16,128]{0,2,1:T(8,128)(2,1)S(1)} %collective-permute-done.1) | copy-start | bytes 786436
  105.8 13.6 %collective-permute-start.2 = (bf16[64,64,16]{0,2,1:T(8,128)(2,1)}, bf16[64,64,16]{0,2,1:T(8,128)(2,1)S(1)}, u32[]{:S(2)}, u32[]{:S(2)}) collective-permute-start(bf16[64,64,16]{0,2,1:T(8,128)(2,1)} %get-tuple-element.7), channel_id=1, source_target_pairs={{0,1},{1,2},{2,3},{4,5},{5,6},{6,7},{8,9},{9,10},{10,11},{12,13},{... | collective-permute-start | bytes 393224 | tf_op jit(solution)/shard_map/ppermute | solution.py:18
  107.7 11.7 %collective-permute-start.3 = (bf16[64,64,16]{0,2,1:T(8,128)(2,1)}, bf16[64,64,16]{0,2,1:T(8,128)(2,1)}, u32[]{:S(2)}, u32[]{:S(2)}) collective-permute-start(bf16[64,64,16]{0,2,1:T(8,128)(2,1)} %get-tuple-element.8), channel_id=1, source_target_pairs={{1,0},{2,1},{3,2},{5,4},{6,5},{7,6},{9,8},{10,9},{11,10},{13,12},{... | collective-permute-start | bytes 393224 | tf_op jit(solution)/shard_map/ppermute | solution.py:19
  114.3 25.1 %all-to-all-start.1 = ((f32[4,20,4096]{2,1,0:T(8,128)}), f32[4,20,4096]{2,1,0:T(8,128)S(1)}, u32[]{:S(2)}, u32[]{:S(2)}) async-start(f32[4,20,4096]{2,1,0:T(8,128)} %convolution_bitcast_fusion), calls=%async_computation.1 | async-start | bytes 3145728 | tf_op jit(solution)/shard_map/all_to_all | solution.py:109
  139.6 1.0 copy-start.4
where the time goes:
time: 152 us; the launch traced here: 151 us
  waiting for transfers between devices  52.6 us (35%)
  local copies, waits for them, and re-layouts  47.2 us (31%)
  matrix products  23 us (15%)
  starting transfers between devices  21.5 us (14%)
  other arithmetic  6.1 us (4%)
    ppermute x2, waiting for transfers between devices, extended(): before = lax.ppermute(last, axis, up)  47.8 us
    dot_general x1, matrix products, body(): jnp.einsum('srt,stv->srv', coupling[0], sources, precision=precise)  8.83 us
    all_to_all x1, starting transfers between devices, body(): lax.all_to_all(outgoing, 'qx', split_axis=0, concat_axis=0, tiled=True)  6.3 us
    dot_general x1, matrix products, body(): jnp.einsum('ijkps,ijkvs->ijvp', near_tiles, picked, preferred_element_typ...  5.76 us
    squeeze x1, local copies, waits for them, and re-layouts, body(): coupling[0]  5.56 us
    dot_general x1, local copies, waits for them, and re-layouts, body(): jnp.einsum('srt,stv->srv', coupling[0], sources, precision=precise)  5.33 us
    ppermute x2, starting transfers between devices, extended(): before = lax.ppermute(last, axis, up)  5.28 us
    dot_general x1, matrix products, body(): jnp.einsum('ajcn,ajcf->jnf', arrival, first_hop, precision=precise)  5.26 us
  transfers between devices with their start and end apart: 6, of which 2 were waited for; matrix products, arithmetic and copies ran while one was open for 16% of the time, Pallas kernels for 0%

commit v1 on v0

v1 whole, which is shorter than its diff:
```python
import jax
import jax.numpy as jnp
from jax import lax
from jax.experimental import pallas as pl
from jax.experimental.pallas import tpu as pltpu
from jax.sharding import PartitionSpec as P

LS = 16
K0 = 6
K1 = 8


def extended(array, sides, width):
    for axis, dim in sides:
        peers, length = (lax.axis_size(axis), array.shape[dim])
        up = [(i, (i + 1) % peers) for i in range(peers - 1)]
        down = [(j, i) for i, j in up]
        last = lax.slice_in_dim(array, length - width, length, axis=dim)
        initial = lax.slice_in_dim(array, 0, width, axis=dim)
        before = lax.ppermute(last, axis, up)
        after = lax.ppermute(initial, axis, down)
        array = jnp.concatenate([before, array, after], axis=dim)
    return array


VM = pl.BlockSpec(memory_space=pltpu.VMEM)
SM = pl.BlockSpec(memory_space=pltpu.SMEM)
TOP = 14


def halves(value):
    high = value.astype(jnp.bfloat16)
    return high, (value - high.astype(jnp.float32)).astype(jnp.bfloat16)


def product_of(left, right):
    lh, ll = halves(left)
    rh, rl = halves(right)
    return jnp.dot(
        jnp.concatenate([lh, ll, lh, ll], axis=1),
        jnp.concatenate([rh, rh, rl, rl], axis=0),
        preferred_element_type=jnp.float32,
    )


def contrib_kernel(leaf_count, upper_count, pos_ref, coup_ref, leaf_ref, upper_ref, out_ref, max_ref):
    rank = coup_ref.shape[1]
    half = rank // 2
    out_ref[...] = jnp.zeros_like(out_ref)
    max_ref[...] = jnp.zeros_like(max_ref)

    def group(first, count, coef):
        mats = coup_ref[pl.ds(first, count)].reshape(count * rank, rank)
        res = product_of(mats, coef)
        for q in range(count):
            row = pos_ref[first + q]
            one = res[q * rank : (q + 1) * rank]
            folded = jnp.concatenate([one[:half], one[half:]], axis=1)
            out_ref[row] = folded
            max_ref[row] = jnp.max(jnp.abs(folded), axis=0, keepdims=True)

    def leaf_step(m, carry):
        group(m * K0, K0, leaf_ref[m])
        return carry

    def upper_step(m, carry):
        group(leaf_count * K0 + m * K1, K1, upper_ref[m])
        return carry

    lax.fori_loop(0, leaf_count, leaf_step, 0)
    lax.fori_loop(0, upper_count, upper_step, 0)


def near_kernel(leaf_y, off_ref, tiles_ref, grid_ref, out_ref):
    m = pl.program_id(0)
    i = m // leaf_y
    j = lax.rem(m, leaf_y)
    vecs = grid_ref.shape[2]
    total = None
    for k in range(tiles_ref.shape[1]):
        o = off_ref[m, k]
        x = (i + o // 3) * LS
        y = pl.multiple_of((j + lax.rem(o, 3)) * LS, LS)
        block = grid_ref[pl.ds(x, LS), pl.ds(y, LS), :].reshape(LS * LS, vecs)
        term = jnp.dot(tiles_ref[0, k], block, preferred_element_type=jnp.float32)
        total = term if total is None else total + term
    out_ref[0] = total


def far_kernel(leaf_x, leaf_y, tgt_ref, recv_ref, down_ref, row_ref, near_ref, out_ref, acc, full):
    leaf_count = leaf_x * leaf_y
    half = acc.shape[2] // 2
    acc[...] = jnp.zeros_like(acc)

    def add(r, carry):
        t = tgt_ref[r]
        acc[t] = acc[t] + recv_ref[r]
        return carry

    lax.fori_loop(0, recv_ref.shape[0], add, 0, unroll=4)

    def unfolded(n):
        value = acc[n]
        return jnp.concatenate([value[:, :half], value[:, half:]], axis=0)

    def leaf(m, carry):
        j = lax.rem(m, leaf_y)
        coef = unfolded(m) + product_of(down_ref[m], unfolded(leaf_count + j // 2))
        high, low = halves(coef)
        basis = row_ref[m]
        far = lax.dot_general(
            jnp.concatenate([basis, basis], axis=0),
            jnp.concatenate([high, low], axis=0),
            (((0,), (0,)), ((), ())),
            preferred_element_type=jnp.float32,
        )
        full[m] = near_ref[m] + far
        return carry

    lax.fori_loop(0, leaf_count, leaf, 0)
    for a in range(leaf_x):
        for i in range(LS):
            rows = [full[a * leaf_y + h, i * LS : (i + 1) * LS, :] for h in range(leaf_y)]
            out_ref[:, a * LS + i, :] = jnp.concatenate(rows, axis=0).T


def body(
    vectors,
    near_tiles,
    near_offset,
    col_basis,
    row_basis,
    up_transfer,
    down_transfer,
    coupling,
    couple_dest,
    couple_target,
):
    precise = lax.Precision.HIGHEST
    f32 = jnp.float32
    shape = jax.ShapeDtypeStruct
    width_x = lax.axis_size("qx")
    width_y = lax.axis_size("qy")
    devices = width_x * width_y
    vec_count, rows_x, rows_y = vectors.shape
    leaf_x = rows_x // LS
    leaf_y = rows_y // LS
    leaf_count = leaf_x * leaf_y
    upper_count = leaf_y // 2
    cluster_count = leaf_count + upper_count
    rank_size = coupling.shape[2]
    slot_count = coupling.shape[1]
    capacity = (slot_count + devices - 1) // devices
    near_count = near_tiles.shape[2]
    points = LS * LS
    fold = (rank_size // 2, 2 * vec_count)
    my_index = lax.axis_index("qx") * width_y + lax.axis_index("qy")

    padded = extended(vectors, (("qx", 1), ("qy", 2)), LS)

    blocks = (
        vectors.reshape(vec_count, leaf_x, LS, leaf_y, LS)
        .transpose(1, 3, 0, 2, 4)
        .reshape(leaf_x, leaf_y, vec_count, points)
    )
    leaf_coef = jnp.einsum("ijrp,ijvp->ijrv", col_basis, blocks, preferred_element_type=f32)
    lifted = jnp.einsum("ijrs,ijsv->ijrv", up_transfer, leaf_coef, precision=precise)
    upper_coef = lifted.reshape(leaf_x, upper_count, 2, rank_size, vec_count).sum(axis=(0, 2))

    own_dest = lax.dynamic_index_in_dim(couple_dest, my_index, 0, keepdims=False)
    slot_ident = jnp.arange(slot_count, dtype=jnp.int32)
    same_dest = own_dest[:, None] == own_dest[None, :]
    earlier = slot_ident[:, None] > slot_ident[None, :]
    order_in = jnp.sum((same_dest & earlier).astype(jnp.int32), axis=1)
    spare_row = devices * capacity
    position = jnp.where(own_dest >= 0, own_dest * capacity + order_in, spare_row)
    placed, peaks = pl.pallas_call(
        lambda *refs: contrib_kernel(leaf_count, upper_count, *refs),
        out_shape=(shape((spare_row + 1,) + fold, f32), shape((spare_row + 1, 1, fold[1]), f32)),
        in_specs=[SM, VM, VM, VM],
        out_specs=(VM, VM),
        name="contrib",
    )(position, coupling[0], leaf_coef.reshape(leaf_count, rank_size, vec_count), upper_coef)

    peak = jnp.max(peaks[:spare_row], axis=(1, 2))
    power = jnp.ceil(jnp.log2(jnp.maximum(peak, 1e-30)))
    scaled = placed[:spare_row] * jnp.exp2(TOP - power)[:, None, None]
    notes = jnp.broadcast_to(power.reshape(devices, capacity, 1), (devices, capacity, fold[1]))
    outgoing = jnp.concatenate(
        [
            scaled.reshape(devices, capacity * fold[0], fold[1]).astype(jnp.float16),
            notes.astype(jnp.float16),
        ],
        axis=1,
    )
    outgoing, padded = lax.optimization_barrier((outgoing, padded))
    arrived = lax.all_to_all(outgoing, ("qx", "qy"), split_axis=0, concat_axis=0, tiled=True)

    grid = padded.transpose(1, 2, 0)
    near = pl.pallas_call(
        lambda *refs: near_kernel(leaf_y, *refs),
        grid=(leaf_count,),
        out_shape=shape((leaf_count, points, vec_count), f32),
        in_specs=[
            SM,
            pl.BlockSpec((1, near_count, points, points), lambda m: (m, 0, 0, 0)),
            VM,
        ],
        out_specs=pl.BlockSpec((1, points, vec_count), lambda m: (m, 0, 0)),
        cost_estimate=pl.CostEstimate(
            flops=2 * leaf_count * near_count * points * points * vec_count,
            bytes_accessed=leaf_count * near_count * points * points * 2,
            transcendentals=0,
        ),
        name="near",
    )(
        near_offset.reshape(leaf_count, near_count),
        near_tiles.reshape(leaf_count, near_count, points, points),
        grid,
    )

    matches = couple_dest == my_index
    counts = matches.astype(jnp.int32)
    order = jnp.cumsum(counts, axis=-1) - counts
    landing = matches[:, None, :] & (order[:, None, :] == jnp.arange(capacity, dtype=jnp.int32)[None, :, None])
    target = cluster_count + jnp.sum(
        jnp.where(landing, couple_target[:, None, :] - cluster_count, 0), axis=-1
    )

    rows = capacity * fold[0]
    exponent = arrived[:, rows:, :1].astype(f32).reshape(spare_row, 1, 1)
    recv = arrived[:, :rows].astype(f32).reshape((spare_row,) + fold) * jnp.exp2(exponent - TOP)
    return pl.pallas_call(
        lambda *refs: far_kernel(leaf_x, leaf_y, *refs),
        out_shape=shape((vec_count, rows_x, rows_y), f32),
        in_specs=[SM, VM, VM, VM, VM],
        out_specs=VM,
        scratch_shapes=[
            pltpu.VMEM((cluster_count + 1,) + fold, f32),
            pltpu.VMEM((leaf_count, points, vec_count), f32),
        ],
        name="far",
    )(
        target.reshape(spare_row),
        recv,
        down_transfer.reshape(leaf_count, rank_size, rank_size),
        row_basis.reshape(leaf_count, rank_size, points),
        near,
    )


def solution(mesh):
    return jax.shard_map(
        body,
        mesh=mesh,
        in_specs=(
            P(None, "qx", "qy"),
            P("qx", "qy", None, None, None),
            P("qx", "qy", None),
            P("qx", "qy", None, None),
            P("qx", "qy", None, None),
            P("qx", "qy", None, None),
            P("qx", "qy", None, None),
            P(("qx", "qy"), None, None, None),
            P(),
            P(),
        ),
        out_specs=P(None, "qx", "qy"),
        check_vma=False,
    )
```

time: 152 us -> 95.8 us (0.63)
  the two profiles are of different devices: /device:TPU:16 before, /device:TPU:0 now
where the time goes in v1:
time: 95.8 us; the launch traced here: 95.1 us
  Pallas kernels  34.6 us (36%)
  starting transfers between devices  19.4 us (20%)
  waiting for transfers between devices  15 us (16%)
  local copies, waits for them, and re-layouts  11.7 us (12%)
  other arithmetic  11.6 us (12%)
  matrix products  2.64 us (3%)
    pallas_call x1, Pallas kernels, body(): pl.pallas_call(lambda *refs: near_kernel(leaf_y, *refs), grid=(leaf_count...  13 us
    all_to_all x1, waiting for transfers between devices, body(): lax.all_to_all(outgoing, ('qx', 'qy'), split_axis=0, concat_axis=0, tiled...  12.8 us
    pallas_call x1, Pallas kernels, body(): pl.pallas_call(lambda *refs: far_kernel(leaf_x, leaf_y, *refs), out_shape...  11 us
    pallas_call x1, Pallas kernels, body(): pl.pallas_call(lambda *refs: contrib_kernel(leaf_count, upper_count, *ref...  10.6 us
    all_to_all x1, starting transfers between devices, body(): lax.all_to_all(outgoing, ('qx', 'qy'), split_axis=0, concat_axis=0, tiled...  10.4 us
    unnamed x13, local copies, waits for them, and re-layouts  7.48 us
    ppermute x2, starting transfers between devices, extended(): before = lax.ppermute(last, axis, up)  6.39 us
    concatenate x1, other arithmetic, extended(): array = jnp.concatenate([before, array, after], axis=dim)  3.64 us
  transfers between devices with their start and end apart: 5, of which 2 were waited for; matrix products, arithmetic and copies ran while one was open for 18% of the time, Pallas kernels for 25%

profile of v1, /device:TPU:0, one launch (start us, length us, event | category | flops | bytes accessed | tf_op | source)
XLA Modules:
  0.0 95.1 jit_solution(10260365476252779901)
XLA Ops:
  0.0 1.8 %copy.56 = bf16[64,32,128]{0,2,1:T(8,128)(2,1)S(1)} copy(bf16[64,32,128]{2,1,0:T(8,128)(2,1)} %param.10) | data formatting | bytes 1048576 | tf_op args[0]
  1.8 1.1 %fusion.4 = (bf16[64,16,128]{0,2,1:T(8,128)(2,1)}, bf16[64,16,128]{0,2,1:T(8,128)(2,1)}) fusion(bf16[64,32,128]{0,2,1:T(8,128)(2,1)S(1)} %copy.56), kind=kLoop, calls=%fused_computation.25 | loop fusion | bytes 1048576 | tf_op jit(solution)/shard_map/slice | solution.py:18
  2.9 4.9 %collective-permute-start = (bf16[64,16,128]{0,2,1:T(8,128)(2,1)}, bf16[64,16,128]{0,2,1:T(8,128)(2,1)S(1)}, u32[]{:S(2)}, u32[]{:S(2)}) collective-permute-start(bf16[64,16,128]{0,2,1:T(8,128)(2,1)} %get-tuple-element.17), channel_id=1, source_target_pairs={{0,4},{4,8},{8,12},{12,16},{16,20},{20,24},{24,28},{1,5},{5,9},{9,... | collective-permute-start | bytes 786440 | tf_op jit(solution)/shard_map/ppermute | solution.py:20
  7.8 1.3 %collective-permute-start.1 = (bf16[64,16,128]{0,2,1:T(8,128)(2,1)}, bf16[64,16,128]{0,2,1:T(8,128)(2,1)S(1)}, u32[]{:S(2)}, u32[]{:S(2)}) collective-permute-start(bf16[64,16,128]{0,2,1:T(8,128)(2,1)} %get-tuple-element.18), channel_id=1, source_target_pairs={{4,0},{8,4},{12,8},{16,12},{20,16},{24,20},{28,24},{5,1},{9,5},{13... | collective-permute-start | bytes 786440 | tf_op jit(solution)/shard_map/ppermute | solution.py:21
  9.4 0.6 compare_select_fusion.refs_0_
  10.2 0.3 fusion.5
  10.5 2.3 %fusion.6 = f32[8,64,64,1]{2,1,0,3:T(8,128)S(1)} fusion(f32[2,8,64,64]{3,2,1,0:T(8,128)S(1)} %fusion.5, f32[2,8,64,64]{3,2,1,0:T(8,128)} %param.15), kind=kOutput, calls=%fused_computation.27 | convolution fusion | flops 50331648 | bytes 655360 | tf_op jit(solution)/shard_map/ijrs,ijsv->ijrv/dot_general | solution.py:167
  12.9 0.7 copy.60.refs_3_
  13.6 5.6 %copy.55 = f32[1,128,64,64]{3,2,1,0:T(8,128)} copy(f32[1,128,64,64]{1,3,2,0:T(8,128)} %param.17) | data formatting | bytes 4194304 | tf_op args[7]
  19.2 10.6 %contrib.1 = (f32[129,32,128]{2,1,0:T(8,128)}, f32[129,1,128]{2,1,0:T(1,128)}) custom-call(s32[128]{0:T(128)} %compare_select_fusion.refs_0_, f32[128,64,64]{2,1,0:T(8,128)} %bitcast.30, f32[16,64,64]{2,1,0:T(8,128)} %bitcast.33, f32[4,64,64]{2,1,0:T(8,128)} %copy.60.refs_3_), custom_call_target="tpu_custom_call" | custom-call | tf_op jit(solution)/shard_map/contrib/pallas_call | solution.py:177
  29.8 1.9 %slice_reduce_fusion = f32[128]{0:T(128)S(1)} fusion(f32[129,1,128]{2,1,0:T(1,128)} %get-tuple-element.10), kind=kLoop, calls=%fused_computation.7 | loop fusion | flops 16256 | bytes 66048 | tf_op jit(solution)/shard_map/reduce_max | solution.py:185
  31.8 1.9 %multiply_convert_fusion = f16[128,32,128]{2,1,0:T(8,128)(2,1)S(1)} fusion(f32[129,32,128]{2,1,0:T(8,128)} %get-tuple-element.9, f32[128]{0:T(128)S(1)} %get-tuple-element.19), kind=kLoop, calls=%fused_computation.2 | loop fusion | flops 1048576 | bytes 3146240 | tf_op jit(solution)/shard_map/convert_element_type | solution.py:191
  33.8 1.5 %collective-permute-start.2 = (bf16[64,64,16]{0,2,1:T(8,128)(2,1)S(1)}, bf16[64,64,16]{0,2,1:T(8,128)(2,1)S(1)}, u32[]{:S(2)}, u32[]{:S(2)}) collective-permute-start(bf16[64,64,16]{0,2,1:T(8,128)(2,1)S(1)} %get-tuple-element.15), channel_id=1, source_target_pairs={{0,1},{1,2},{2,3},{4,5},{5,6},{6,7},{8,9},{9,10},{10,11},{12,13},{... | collective-permute-start | bytes 393224 | tf_op jit(solution)/shard_map/ppermute | solution.py:20
  35.3 1.3 %collective-permute-start.3 = (bf16[64,64,16]{0,2,1:T(8,128)(2,1)S(1)}, bf16[64,64,16]{0,2,1:T(8,128)(2,1)S(1)}, u32[]{:S(2)}, u32[]{:S(2)}) collective-permute-start(bf16[64,64,16]{0,2,1:T(8,128)(2,1)S(1)} %get-tuple-element.16), channel_id=1, source_target_pairs={{1,0},{2,1},{3,2},{5,4},{6,5},{7,6},{9,8},{10,9},{11,10},{13,12},{... | collective-permute-start | bytes 393224 | tf_op jit(solution)/shard_map/ppermute | solution.py:21
  36.7 1.3 %pad_maximum_fusion.1 = f16[32,132,128]{2,1,0:T(8,128)(2,1)} fusion(f16[32,4,128]{2,1,0:T(4,128)(2,1)S(1)} %broadcast_in_dim.17, f16[32,128,128]{2,1,0:T(8,128)(2,1)S(1)} %bitcast.34), kind=kLoop, calls=%fused_computation.3 | loop fusion | flops 540672 | bytes 2162688 | tf_op jit(solution)/shard_map/concatenate | solution.py:189
  38.1 2.2 %collective-permute-done.3 = bf16[64,64,16]{0,2,1:T(8,128)(2,1)S(1)} collective-permute-done((bf16[64,64,16]{0,2,1:T(8,128)(2,1)S(1)}, bf16[64,64,16]{0,2,1:T(8,128)(2,1)S(1)}, u32[]{:S(2)}, u32[]{:S(2)}) %collective-permute-start.3) | collective-permute-done | bytes 131104 | tf_op jit(solution)/shard_map/ppermute | solution.py:21
  40.3 3.6 %pad_maximum_fusion = bf16[64,64,160]{0,2,1:T(8,128)(2,1)} fusion(bf16[64,64,16]{0,2,1:T(8,128)(2,1)S(1)} %collective-permute-done.3, bf16[64,16,128]{0,2,1:T(8,128)(2,1)S(1)} %collective-permute-done.1, bf16[64,32,128]{0,2,1:T(8,128)(2,1)S(1)} %copy.56, bf16[64,16,128]{0,2,1:T(8,128)(2,1)S(1)} %collective-permute-done, ...), kind=kLoop, calls=%fused_computation | loop fusion | flops 6553600 | bytes 2621440 | tf_op jit(solution)/shard_map/concatenate | solution.py:22
  43.9 10.4 %all-to-all-start = ((f16[32,132,128]{2,1,0:T(8,128)(2,1)}), f16[32,132,128]{2,1,0:T(8,128)(2,1)S(1)}, u32[]{:S(2)}, u32[]{:S(2)}) async-start(f16[32,132,128]{2,1,0:T(8,128)(2,1)} %pad_maximum_fusion.1), calls=%async_computation | async-start | bytes 2228224 | tf_op jit(solution)/shard_map/all_to_all | solution.py:197
  54.3 0.7 copy.69
  55.6 0.6 add.32.refs_0_
  56.2 13.0 %near.1.refs_4_ = f32[16,256,64]{2,1,0:T(8,128)} custom-call(s32[16,3]{1,0:T(8,128)} %bitcast.40, bf16[16,3,256,256]{3,2,1,0:T(8,128)(2,1)} %bitcast.32, bf16[64,160,64]{2,1,0:T(8,128)(2,1)} %bitcast.31), custom_call_target="tpu_custom_call" | custom-call | flops 402653184 | bytes 6291456 | tf_op jit(solution)/shard_map/near/pallas_call | solution.py:200
  69.2 12.8 %all-to-all-done = f16[32,132,128]{2,1,0:T(8,128)(2,1)S(1)} async-done(((f16[32,132,128]{2,1,0:T(8,128)(2,1)}), f16[32,132,128]{2,1,0:T(8,128)(2,1)S(1)}, u32[]{:S(2)}, u32[]{:S(2)}) %all-to-all-start) | async-done | bytes 1081376 | tf_op jit(solution)/shard_map/all_to_all | solution.py:197
  82.6 1.5 %convert_multiply_fusion.refs_1_ = f32[128,32,128]{2,1,0:T(8,128)} fusion(f16[128,32,128]{2,1,0:T(8,128)(2,1)S(1)} %bitcast.35, f32[128]{0:T(128)S(1)} %exp2.46), kind=kLoop, calls=%fused_computation.1 | loop fusion | flops 1048576 | bytes 3146240 | tf_op jit(solution)/shard_map/mul | solution.py:232
  84.1 11.0 %far.1 = f32[64,32,128]{2,1,0:T(8,128)} custom-call(s32[128]{0:T(128)} %add.32.refs_0_, f32[128,32,128]{2,1,0:T(8,128)} %convert_multiply_fusion.refs_1_, f32[16,64,64]{2,1,0:T(8,128)} %bitcast.38, bf16[16,64,256]{2,1,0:T(8,128)(2,1)} %bitcast.39, f32[16,256,64]{2,1,0:T(8,128)} %near.1.refs_4_), custom_call_target="tpu_custom_call" | custom-call | tf_op jit(solution)/shard_map/far/pallas_call | solution.py:233
  (33 shorter events, 2.0 us)
Async XLA Ops:
  0.0 10.2 %copy-start = (bf16[2,8,64,256]{3,2,1,0:T(8,128)(2,1)S(1)}, bf16[2,8,64,256]{3,2,1,0:T(8,128)(2,1)}, u32[]{:S(2)}) copy-start(bf16[2,8,64,256]{3,2,1,0:T(8,128)(2,1)} %param.13) | copy-start | bytes 1572868
  0.0 9.1 %copy-start.2 = (s32[32,128]{1,0:T(8,128)S(1)}, s32[32,128]{1,0:T(8,128)}, u32[]{:S(2)}) copy-start(s32[32,128]{1,0:T(8,128)} %param.18) | copy-start | bytes 49156
  2.9 30.8 %collective-permute-start = (bf16[64,16,128]{0,2,1:T(8,128)(2,1)}, bf16[64,16,128]{0,2,1:T(8,128)(2,1)S(1)}, u32[]{:S(2)}, u32[]{:S(2)}) collective-permute-start(bf16[64,16,128]{0,2,1:T(8,128)(2,1)} %get-tuple-element.17), channel_id=1, source_target_pairs={{0,4},{4,8},{8,12},{12,16},{16,20},{20,24},{24,28},{1,5},{5,9},{9,... | collective-permute-start | bytes 786440 | tf_op jit(solution)/shard_map/ppermute | solution.py:20
  7.8 25.9 %collective-permute-start.1 = (bf16[64,16,128]{0,2,1:T(8,128)(2,1)}, bf16[64,16,128]{0,2,1:T(8,128)(2,1)S(1)}, u32[]{:S(2)}, u32[]{:S(2)}) collective-permute-start(bf16[64,16,128]{0,2,1:T(8,128)(2,1)} %get-tuple-element.18), channel_id=1, source_target_pairs={{4,0},{8,4},{12,8},{16,12},{20,16},{24,20},{28,24},{5,1},{9,5},{13... | collective-permute-start | bytes 786440 | tf_op jit(solution)/shard_map/ppermute | solution.py:21
  10.5 8.7 %copy-start.1 = (f32[2,8,64,64]{3,2,1,0:T(8,128)}, f32[2,8,64,64]{3,2,1,0:T(8,128)S(1)}, u32[]{:S(2)}) copy-start(f32[2,8,64,64]{3,2,1,0:T(8,128)S(1)} %fusion.5) | copy-start | bytes 786436
  33.8 4.2 %collective-permute-start.2 = (bf16[64,64,16]{0,2,1:T(8,128)(2,1)S(1)}, bf16[64,64,16]{0,2,1:T(8,128)(2,1)S(1)}, u32[]{:S(2)}, u32[]{:S(2)}) collective-permute-start(bf16[64,64,16]{0,2,1:T(8,128)(2,1)S(1)} %get-tuple-element.15), channel_id=1, source_target_pairs={{0,1},{1,2},{2,3},{4,5},{5,6},{6,7},{8,9},{9,10},{10,11},{12,13},{... | collective-permute-start | bytes 393224 | tf_op jit(solution)/shard_map/ppermute | solution.py:20
  35.3 5.0 %collective-permute-start.3 = (bf16[64,64,16]{0,2,1:T(8,128)(2,1)S(1)}, bf16[64,64,16]{0,2,1:T(8,128)(2,1)S(1)}, u32[]{:S(2)}, u32[]{:S(2)}) collective-permute-start(bf16[64,64,16]{0,2,1:T(8,128)(2,1)S(1)} %get-tuple-element.16), channel_id=1, source_target_pairs={{1,0},{2,1},{3,2},{5,4},{6,5},{7,6},{9,8},{10,9},{11,10},{13,12},{... | collective-permute-start | bytes 393224 | tf_op jit(solution)/shard_map/ppermute | solution.py:21
  38.0 16.3 %copy-start.4 = (s32[2,8,3]{1,0,2:T(2,128)S(1)}, s32[2,8,3]{1,0,2:T(2,128)}, u32[]{:S(2)}) copy-start(s32[2,8,3]{1,0,2:T(2,128)} %param.12) | copy-start | bytes 580
  38.0 17.3 %copy-start.3 = (s32[32,128]{1,0:T(8,128)S(1)}, s32[32,128]{1,0:T(8,128)}, u32[]{:S(2)}) copy-start(s32[32,128]{1,0:T(8,128)} %param.19) | copy-start | bytes 49156
  43.9 38.0 %all-to-all-start = ((f16[32,132,128]{2,1,0:T(8,128)(2,1)}), f16[32,132,128]{2,1,0:T(8,128)(2,1)S(1)}, u32[]{:S(2)}, u32[]{:S(2)}) async-start(f16[32,132,128]{2,1,0:T(8,128)(2,1)} %pad_maximum_fusion.1), calls=%async_computation | async-start | bytes 2228224 | tf_op jit(solution)/shard_map/all_to_all | solution.py:197

commit v2 on v1

--- a/solution.py
+++ b/solution.py
@@ -10,17 +10,13 @@
 K1 = 8
 
 
-def extended(array, sides, width):
-    for axis, dim in sides:
-        peers, length = (lax.axis_size(axis), array.shape[dim])
-        up = [(i, (i + 1) % peers) for i in range(peers - 1)]
-        down = [(j, i) for i, j in up]
-        last = lax.slice_in_dim(array, length - width, length, axis=dim)
-        initial = lax.slice_in_dim(array, 0, width, axis=dim)
-        before = lax.ppermute(last, axis, up)
-        after = lax.ppermute(initial, axis, down)
-        array = jnp.concatenate([before, array, after], axis=dim)
-    return array
+def edges(array, axis, dim, width):
+    peers, length = (lax.axis_size(axis), array.shape[dim])
+    up = [(i, (i + 1) % peers) for i in range(peers - 1)]
+    down = [(j, i) for i, j in up]
+    last = lax.slice_in_dim(array, length - width, length, axis=dim)
+    initial = lax.slice_in_dim(array, 0, width, axis=dim)
+    return [lax.ppermute(last, axis, up), array, lax.ppermute(initial, axis, down)]
 
 
 VM = pl.BlockSpec(memory_space=pltpu.VMEM)
@@ -57,7 +53,7 @@
             one = res[q * rank : (q + 1) * rank]
             folded = jnp.concatenate([one[:half], one[half:]], axis=1)
             out_ref[row] = folded
-            max_ref[row] = jnp.max(jnp.abs(folded), axis=0, keepdims=True)
+            max_ref[pl.ds(row, 1), :] = jnp.max(jnp.abs(folded), axis=0, keepdims=True)
 
     def leaf_step(m, carry):
         group(m * K0, K0, leaf_ref[m])
@@ -67,8 +63,8 @@
         group(leaf_count * K0 + m * K1, K1, upper_ref[m])
         return carry
 
-    lax.fori_loop(0, leaf_count, leaf_step, 0)
-    lax.fori_loop(0, upper_count, upper_step, 0)
+    lax.fori_loop(0, leaf_count, leaf_step, 0, unroll=4)
+    lax.fori_loop(0, upper_count, upper_step, 0, unroll=2)
 
 
 def near_kernel(leaf_y, off_ref, tiles_ref, grid_ref, out_ref):
@@ -117,7 +113,7 @@
         full[m] = near_ref[m] + far
         return carry
 
-    lax.fori_loop(0, leaf_count, leaf, 0)
+    lax.fori_loop(0, leaf_count, leaf, 0, unroll=4)
     for a in range(leaf_x):
         for i in range(LS):
             rows = [full[a * leaf_y + h, i * LS : (i + 1) * LS, :] for h in range(leaf_y)]
@@ -156,7 +152,8 @@
     fold = (rank_size // 2, 2 * vec_count)
     my_index = lax.axis_index("qx") * width_y + lax.axis_index("qy")
 
-    padded = extended(vectors, (("qx", 1), ("qy", 2)), LS)
+    tall = jnp.concatenate(edges(vectors, "qx", 1, LS), axis=1)
+    pieces = edges(tall, "qy", 2, LS)
 
     blocks = (
         vectors.reshape(vec_count, leaf_x, LS, leaf_y, LS)
@@ -176,13 +173,18 @@
     position = jnp.where(own_dest >= 0, own_dest * capacity + order_in, spare_row)
     placed, peaks = pl.pallas_call(
         lambda *refs: contrib_kernel(leaf_count, upper_count, *refs),
-        out_shape=(shape((spare_row + 1,) + fold, f32), shape((spare_row + 1, 1, fold[1]), f32)),
+        out_shape=(shape((spare_row + 1,) + fold, f32), shape((spare_row + 1, fold[1]), f32)),
         in_specs=[SM, VM, VM, VM],
         out_specs=(VM, VM),
+        cost_estimate=pl.CostEstimate(
+            flops=8 * slot_count * rank_size * rank_size * vec_count,
+            bytes_accessed=16 * slot_count * rank_size * rank_size * 4,
+            transcendentals=0,
+        ),
         name="contrib",
     )(position, coupling[0], leaf_coef.reshape(leaf_count, rank_size, vec_count), upper_coef)
 
-    peak = jnp.max(peaks[:spare_row], axis=(1, 2))
+    peak = jnp.max(peaks[:spare_row], axis=1)
     power = jnp.ceil(jnp.log2(jnp.maximum(peak, 1e-30)))
     scaled = placed[:spare_row] * jnp.exp2(TOP - power)[:, None, None]
     notes = jnp.broadcast_to(power.reshape(devices, capacity, 1), (devices, capacity, fold[1]))
@@ -193,10 +195,10 @@
         ],
         axis=1,
     )
-    outgoing, padded = lax.optimization_barrier((outgoing, padded))
+    outgoing, pieces = lax.optimization_barrier((outgoing, pieces))
     arrived = lax.all_to_all(outgoing, ("qx", "qy"), split_axis=0, concat_axis=0, tiled=True)
 
-    grid = padded.transpose(1, 2, 0)
+    grid = jnp.concatenate([piece.transpose(1, 2, 0) for piece in pieces], axis=1)
     near = pl.pallas_call(
         lambda *refs: near_kernel(leaf_y, *refs),
         grid=(leaf_count,),

time: 95.8 us -> 89.1 us (0.930)
  Pallas kernels: 34.6 us -> 27 us
  local copies, waits for them, and re-layouts: 11.7 us -> 14.7 us
  matrix products: 2.64 us -> 1.4 us
  other arithmetic: 11.6 us -> 10.6 us
    pallas_call x1, Pallas kernels: 10.6 us -> 6.72 us  [body(): pl.pallas_call(lambda *refs: contrib_kernel(leaf_count, upper_count, *ref...]
    pallas_call x1, Pallas kernels: 11 us -> 7.29 us  [body(): pl.pallas_call(lambda *refs: far_kernel(leaf_x, leaf_y, *refs), out_shape...]
    all_to_all x1, waiting for transfers between devices: 12.8 us -> 10.7 us  [body(): lax.all_to_all(outgoing, ('qx', 'qy'), split_axis=0, concat_axis=0, tiled...]
    unnamed x13 -> x19, local copies, waits for them, and re-layouts: 7.48 us -> 9.3 us
    ppermute x4, waiting for transfers between devices: 2.23 us -> 3.71 us  [the longest x2 2.38 us: edges(): lax.ppermute(initial, axis, down)]
    dot_general x1, matrix products: 2.32 us -> 1.08 us  [body(): jnp.einsum('ijrs,ijsv->ijrv', up_transfer, leaf_coef, precision=precise)]
    slice x1, local copies, waits for them, and re-layouts: 0.28 us -> 1.5 us  [body(): arrived[:, :rows].astype(f32).reshape((spare_row,) + fold)]
    slice x1 -> x2, local copies, waits for them, and re-layouts: 1.12 us -> 0.14 us  [the longest x1 0.1 us: edges(): last = lax.slice_in_dim(array, length - width, length, axis=dim)]
  transfers between devices with their start and end apart: 5 -> 5, of which waited for: 2 -> 3; matrix products, arithmetic and copies ran while one was open for 18% -> 19% of each run, Pallas kernels for 25% -> 22%
where the time goes in v2:
time: 89.1 us; the launch traced here: 88.3 us
  Pallas kernels  27 us (30%)
  starting transfers between devices  20 us (22%)
  local copies, waits for them, and re-layouts  14.7 us (16%)
  waiting for transfers between devices  14.4 us (16%)
  other arithmetic  10.6 us (12%)
  matrix products  1.4 us (2%)
    pallas_call x1, Pallas kernels, body(): pl.pallas_call(lambda *refs: near_kernel(leaf_y, *refs), grid=(leaf_count...  13 us
    all_to_all x1, waiting for transfers between devices, body(): lax.all_to_all(outgoing, ('qx', 'qy'), split_axis=0, concat_axis=0, tiled...  10.7 us
    all_to_all x1, starting transfers between devices, body(): lax.all_to_all(outgoing, ('qx', 'qy'), split_axis=0, concat_axis=0, tiled...  10.4 us
    unnamed x19, local copies, waits for them, and re-layouts  9.3 us
    pallas_call x1, Pallas kernels, body(): pl.pallas_call(lambda *refs: far_kernel(leaf_x, leaf_y, *refs), out_shape...  7.29 us
    ppermute x2, starting transfers between devices, edges(): lax.ppermute(last, axis, up)  7.03 us
    pallas_call x1, Pallas kernels, body(): pl.pallas_call(lambda *refs: contrib_kernel(leaf_count, upper_count, *ref...  6.72 us
    ppermute x2, starting transfers between devices, edges(): lax.ppermute(initial, axis, down)  2.57 us
  transfers between devices with their start and end apart: 5, of which 3 were waited for; matrix products, arithmetic and copies ran while one was open for 19% of the time, Pallas kernels for 22%

profile of v2, /device:TPU:0, one launch (start us, length us, event | category | flops | bytes accessed | tf_op | source)
XLA Modules:
  0.0 88.3 jit_solution(13065999086448327637)
XLA Ops:
  0.0 1.8 %copy.56 = bf16[64,32,128]{0,2,1:T(8,128)(2,1)S(1)} copy(bf16[64,32,128]{2,1,0:T(8,128)(2,1)} %param.10) | data formatting | bytes 1048576 | tf_op args[0]
  1.9 5.7 %collective-permute-start = (bf16[64,16,128]{0,2,1:T(8,128)(2,1)S(1)}, bf16[64,16,128]{0,2,1:T(8,128)(2,1)}, u32[]{:S(2)}, u32[]{:S(2)}) collective-permute-start(bf16[64,16,128]{0,2,1:T(8,128)(2,1)S(1)} %get-tuple-element.21), channel_id=1, source_target_pairs={{0,4},{4,8},{8,12},{12,16},{16,20},{20,24},{24,28},{1,5},{5,9},{9,... | collective-permute-start | bytes 786440 | tf_op jit(solution)/shard_map/ppermute | solution.py:19
  7.6 1.3 %collective-permute-start.1 = (bf16[64,16,128]{0,2,1:T(8,128)(2,1)S(1)}, bf16[64,16,128]{0,2,1:T(8,128)(2,1)}, u32[]{:S(2)}, u32[]{:S(2)}) collective-permute-start(bf16[64,16,128]{0,2,1:T(8,128)(2,1)S(1)} %get-tuple-element.22), channel_id=1, source_target_pairs={{4,0},{8,4},{12,8},{16,12},{20,16},{24,20},{28,24},{5,1},{9,5},{13... | collective-permute-start | bytes 786440 | tf_op jit(solution)/shard_map/ppermute | solution.py:19
  10.8 1.1 %fusion.7 = f32[8,64,64,1]{2,1,0,3:T(8,128)S(1)} fusion(f32[2,8,64,64]{3,2,1,0:T(8,128)S(1)} %fusion.6, f32[2,8,64,64]{3,2,1,0:T(8,128)S(1)} %copy-done.4), kind=kOutput, calls=%fused_computation.26 | convolution fusion | flops 50331648 | bytes 655360 | tf_op jit(solution)/shard_map/ijrs,ijsv->ijrv/dot_general | solution.py:164
  11.9 0.7 copy.60.refs_3_
  12.6 5.6 %copy.55 = f32[1,128,64,64]{3,2,1,0:T(8,128)} copy(f32[1,128,64,64]{1,3,2,0:T(8,128)} %param.17) | data formatting | bytes 4194304 | tf_op args[7]
  18.2 6.7 %contrib.1 = (f32[129,32,128]{2,1,0:T(8,128)}, f32[129,128]{1,0:T(8,128)}) custom-call(s32[128]{0:T(128)} %compare_select_fusion.refs_0_, f32[128,64,64]{2,1,0:T(8,128)} %bitcast.31, f32[16,64,64]{2,1,0:T(8,128)} %bitcast.35, f32[4,64,64]{2,1,0:T(8,128)} %copy.60.refs_3_), custom_call_target="tpu_custom_call" | custom-call | flops 268435456 | bytes 33554432 | tf_op jit(solution)/shard_map/contrib/pallas_call | solution.py:174
  24.9 0.9 %slice_reduce_fusion = f32[128]{0:T(128)S(1)} fusion(f32[129,128]{1,0:T(8,128)} %get-tuple-element.12), kind=kLoop, calls=%fused_computation.5 | loop fusion | flops 16256 | bytes 66048 | tf_op jit(solution)/shard_map/reduce_max | solution.py:187
  26.0 1.9 %multiply_convert_fusion = f16[128,32,128]{2,1,0:T(8,128)(2,1)S(1)} fusion(f32[129,32,128]{2,1,0:T(8,128)} %get-tuple-element.11, f32[128]{0:T(128)S(1)} %get-tuple-element.23), kind=kLoop, calls=%fused_computation.3 | loop fusion | flops 1048576 | bytes 3146240 | tf_op jit(solution)/shard_map/convert_element_type | solution.py:193
  27.9 1.3 %collective-permute-done = bf16[64,16,128]{0,2,1:T(8,128)(2,1)} collective-permute-done((bf16[64,16,128]{0,2,1:T(8,128)(2,1)S(1)}, bf16[64,16,128]{0,2,1:T(8,128)(2,1)}, u32[]{:S(2)}, u32[]{:S(2)}) %collective-permute-start) | collective-permute-done | bytes 262176 | tf_op jit(solution)/shard_map/ppermute | solution.py:19
  29.2 1.7 %pad_maximum_fusion.1 = bf16[64,64,128]{0,2,1:T(8,128)(2,1)S(1)} fusion(bf16[64,16,128]{0,2,1:T(8,128)(2,1)} %collective-permute-done.1, bf16[64,32,128]{0,2,1:T(8,128)(2,1)S(1)} %copy.56, bf16[64,16,128]{0,2,1:T(8,128)(2,1)} %collective-permute-done), kind=kLoop, calls=%fused_computation.1 | loop fusion | flops 1048576 | bytes 2097152 | tf_op jit(solution)/shard_map/concatenate | solution.py:155
  30.9 1.3 %copy-done.1 = bf16[64,64,128]{0,2,1:T(8,128)(2,1)} copy-done((bf16[64,64,128]{0,2,1:T(8,128)(2,1)}, bf16[64,64,128]{0,2,1:T(8,128)(2,1)S(1)}, u32[]{:S(2)}) %copy-start.1) | copy-done | bytes 1048600
  32.3 1.3 %collective-permute-start.2 = (bf16[64,64,16]{0,2,1:T(8,128)(2,1)S(1)}, bf16[64,64,16]{0,2,1:T(8,128)(2,1)S(1)}, u32[]{:S(2)}, u32[]{:S(2)}) collective-permute-start(bf16[64,64,16]{0,2,1:T(8,128)(2,1)S(1)} %get-tuple-element.20), channel_id=1, source_target_pairs={{0,1},{1,2},{2,3},{4,5},{5,6},{6,7},{8,9},{9,10},{10,11},{12,13},{... | collective-permute-start | bytes 393224 | tf_op jit(solution)/shard_map/ppermute | solution.py:19
  33.6 1.3 %collective-permute-start.3 = (bf16[64,64,16]{0,2,1:T(8,128)(2,1)S(1)}, bf16[64,64,16]{0,2,1:T(8,128)(2,1)S(1)}, u32[]{:S(2)}, u32[]{:S(2)}) collective-permute-start(bf16[64,64,16]{0,2,1:T(8,128)(2,1)S(1)} %get-tuple-element.19), channel_id=1, source_target_pairs={{1,0},{2,1},{3,2},{5,4},{6,5},{7,6},{9,8},{10,9},{11,10},{13,12},{... | collective-permute-start | bytes 393224 | tf_op jit(solution)/shard_map/ppermute | solution.py:19
  35.0 1.3 %pad_maximum_fusion.2 = f16[32,132,128]{2,1,0:T(8,128)(2,1)} fusion(f16[32,4,128]{2,1,0:T(4,128)(2,1)S(1)} %broadcast_in_dim.17, f16[32,128,128]{2,1,0:T(8,128)(2,1)S(1)} %bitcast.36), kind=kLoop, calls=%fused_computation.4 | loop fusion | flops 540672 | bytes 2162688 | tf_op jit(solution)/shard_map/concatenate | solution.py:191
  36.3 2.4 %collective-permute-done.3 = bf16[64,64,16]{0,2,1:T(8,128)(2,1)S(1)} collective-permute-done((bf16[64,64,16]{0,2,1:T(8,128)(2,1)S(1)}, bf16[64,64,16]{0,2,1:T(8,128)(2,1)S(1)}, u32[]{:S(2)}, u32[]{:S(2)}) %collective-permute-start.3) | collective-permute-done | bytes 131104 | tf_op jit(solution)/shard_map/ppermute | solution.py:19
  38.7 10.4 %all-to-all-start = ((f16[32,132,128]{2,1,0:T(8,128)(2,1)}), f16[32,132,128]{2,1,0:T(8,128)(2,1)}, u32[]{:S(2)}, u32[]{:S(2)}) async-start(f16[32,132,128]{2,1,0:T(8,128)(2,1)} %pad_maximum_fusion.2), calls=%async_computation | async-start | bytes 2228224 | tf_op jit(solution)/shard_map/all_to_all | solution.py:199
  51.1 2.0 %pad_maximum_fusion.refs_2_ = bf16[64,160,64]{2,1,0:T(8,128)(2,1)} fusion(bf16[64,16,64]{2,1,0:T(8,128)(2,1)S(1)} %bitcast.43, bf16[64,128,64]{2,1,0:T(8,128)(2,1)S(1)} %bitcast.33, bf16[64,16,64]{2,1,0:T(8,128)(2,1)S(1)} %bitcast.42), kind=kLoop, calls=%fused_computation | loop fusion | flops 3932160 | bytes 2621440 | tf_op jit(solution)/shard_map/concatenate | solution.py:201
  53.1 13.0 %near.1.refs_4_ = f32[16,256,64]{2,1,0:T(8,128)} custom-call(s32[16,3]{1,0:T(8,128)} %bitcast.44, bf16[16,3,256,256]{3,2,1,0:T(8,128)(2,1)} %bitcast.34, bf16[64,160,64]{2,1,0:T(8,128)(2,1)} %pad_maximum_fusion.refs_2_), custom_call_target="tpu_custom_call" | custom-call | flops 402653184 | bytes 6291456 | tf_op jit(solution)/shard_map/near/pallas_call | solution.py:202
  66.1 10.7 %all-to-all-done = f16[32,132,128]{2,1,0:T(8,128)(2,1)} async-done(((f16[32,132,128]{2,1,0:T(8,128)(2,1)}), f16[32,132,128]{2,1,0:T(8,128)(2,1)}, u32[]{:S(2)}, u32[]{:S(2)}) %all-to-all-start) | async-done | bytes 1081376 | tf_op jit(solution)/shard_map/all_to_all | solution.py:199
  76.7 0.9 slice.37
  77.9 1.5 %slice.36 = f16[32,128,128]{2,1,0:T(8,128)(2,1)S(1)} slice(f16[32,132,128]{2,1,0:T(8,128)(2,1)} %all-to-all-done), slice={[0:32], [0:128], [0:128]} | slice | bytes 2097152 | tf_op jit(solution)/shard_map/slice | solution.py:234
  79.4 1.6 %convert_multiply_fusion.refs_1_ = f32[128,32,128]{2,1,0:T(8,128)} fusion(f16[128,32,128]{2,1,0:T(8,128)(2,1)S(1)} %bitcast.37, f32[128]{0:T(128)S(1)} %exp2.46), kind=kLoop, calls=%fused_computation.2 | loop fusion | flops 1048576 | bytes 3146240 | tf_op jit(solution)/shard_map/mul | solution.py:234
  81.0 7.3 %far.1 = f32[64,32,128]{2,1,0:T(8,128)} custom-call(s32[128]{0:T(128)} %add.32.refs_0_, f32[128,32,128]{2,1,0:T(8,128)} %convert_multiply_fusion.refs_1_, f32[16,64,64]{2,1,0:T(8,128)} %bitcast.40, bf16[16,64,256]{2,1,0:T(8,128)(2,1)} %bitcast.41, f32[16,256,64]{2,1,0:T(8,128)} %near.1.refs_4_), custom_call_target="tpu_custom_call" | custom-call | tf_op jit(solution)/shard_map/far/pallas_call | solution.py:235
  (40 shorter events, 4.4 us)
Async XLA Ops:
  0.0 10.0 %copy-start = (bf16[2,8,64,256]{3,2,1,0:T(8,128)(2,1)S(1)}, bf16[2,8,64,256]{3,2,1,0:T(8,128)(2,1)}, u32[]{:S(2)}) copy-start(bf16[2,8,64,256]{3,2,1,0:T(8,128)(2,1)} %param.13) | copy-start | bytes 1572868
  0.0 8.9 %copy-start.5 = (s32[32,128]{1,0:T(8,128)S(1)}, s32[32,128]{1,0:T(8,128)}, u32[]{:S(2)}) copy-start(s32[32,128]{1,0:T(8,128)} %param.18) | copy-start | bytes 49156
  1.9 27.3 %collective-permute-start = (bf16[64,16,128]{0,2,1:T(8,128)(2,1)S(1)}, bf16[64,16,128]{0,2,1:T(8,128)(2,1)}, u32[]{:S(2)}, u32[]{:S(2)}) collective-permute-start(bf16[64,16,128]{0,2,1:T(8,128)(2,1)S(1)} %get-tuple-element.21), channel_id=1, source_target_pairs={{0,4},{4,8},{8,12},{12,16},{16,20},{20,24},{24,28},{1,5},{5,9},{9,... | collective-permute-start | bytes 786440 | tf_op jit(solution)/shard_map/ppermute | solution.py:19
  7.6 21.6 %collective-permute-start.1 = (bf16[64,16,128]{0,2,1:T(8,128)(2,1)S(1)}, bf16[64,16,128]{0,2,1:T(8,128)(2,1)}, u32[]{:S(2)}, u32[]{:S(2)}) collective-permute-start(bf16[64,16,128]{0,2,1:T(8,128)(2,1)S(1)} %get-tuple-element.22), channel_id=1, source_target_pairs={{4,0},{8,4},{12,8},{16,12},{20,16},{24,20},{28,24},{5,1},{9,5},{13... | collective-permute-start | bytes 786440 | tf_op jit(solution)/shard_map/ppermute | solution.py:19
  9.7 1.0 %copy-start.4 = (f32[2,8,64,64]{3,2,1,0:T(8,128)S(1)}, f32[2,8,64,64]{3,2,1,0:T(8,128)}, u32[]{:S(2)}) copy-start(f32[2,8,64,64]{3,2,1,0:T(8,128)} %param.15) | copy-start | bytes 786436
  10.8 7.4 %copy-start.3 = (f32[2,8,64,64]{3,2,1,0:T(8,128)}, f32[2,8,64,64]{3,2,1,0:T(8,128)S(1)}, u32[]{:S(2)}) copy-start(f32[2,8,64,64]{3,2,1,0:T(8,128)S(1)} %fusion.6) | copy-start | bytes 786436
  30.9 1.3 %copy-start.1 = (bf16[64,64,128]{0,2,1:T(8,128)(2,1)}, bf16[64,64,128]{0,2,1:T(8,128)(2,1)S(1)}, u32[]{:S(2)}) copy-start(bf16[64,64,128]{0,2,1:T(8,128)(2,1)S(1)} %pad_maximum_fusion.1) | copy-start | bytes 3145732
  32.3 4.1 %collective-permute-start.2 = (bf16[64,64,16]{0,2,1:T(8,128)(2,1)S(1)}, bf16[64,64,16]{0,2,1:T(8,128)(2,1)S(1)}, u32[]{:S(2)}, u32[]{:S(2)}) collective-permute-start(bf16[64,64,16]{0,2,1:T(8,128)(2,1)S(1)} %get-tuple-element.20), channel_id=1, source_target_pairs={{0,1},{1,2},{2,3},{4,5},{5,6},{6,7},{8,9},{9,10},{10,11},{12,13},{... | collective-permute-start | bytes 393224 | tf_op jit(solution)/shard_map/ppermute | solution.py:19
  33.6 5.1 %collective-permute-start.3 = (bf16[64,64,16]{0,2,1:T(8,128)(2,1)S(1)}, bf16[64,64,16]{0,2,1:T(8,128)(2,1)S(1)}, u32[]{:S(2)}, u32[]{:S(2)}) collective-permute-start(bf16[64,64,16]{0,2,1:T(8,128)(2,1)S(1)} %get-tuple-element.19), channel_id=1, source_target_pairs={{1,0},{2,1},{3,2},{5,4},{6,5},{7,6},{9,8},{10,9},{11,10},{13,12},{... | collective-permute-start | bytes 393224 | tf_op jit(solution)/shard_map/ppermute | solution.py:19
  35.0 14.2 %copy-start.7 = (s32[2,8,3]{1,0,2:T(2,128)S(1)}, s32[2,8,3]{1,0,2:T(2,128)}, u32[]{:S(2)}) copy-start(s32[2,8,3]{1,0,2:T(2,128)} %param.12) | copy-start | bytes 580
  35.0 15.1 %copy-start.6 = (s32[32,128]{1,0:T(8,128)S(1)}, s32[32,128]{1,0:T(8,128)}, u32[]{:S(2)}) copy-start(s32[32,128]{1,0:T(8,128)} %param.19) | copy-start | bytes 49156
  35.0 16.1 %copy-start.2 = (bf16[64,64,128]{0,2,1:T(8,128)(2,1)S(1)}, bf16[64,64,128]{0,2,1:T(8,128)(2,1)}, u32[]{:S(2)}) copy-start(bf16[64,64,128]{0,2,1:T(8,128)(2,1)} %copy-done.1) | copy-start | bytes 3145732
  38.7 38.0 %all-to-all-start = ((f16[32,132,128]{2,1,0:T(8,128)(2,1)}), f16[32,132,128]{2,1,0:T(8,128)(2,1)}, u32[]{:S(2)}, u32[]{:S(2)}) async-start(f16[32,132,128]{2,1,0:T(8,128)(2,1)} %pad_maximum_fusion.2), calls=%async_computation | async-start | bytes 2228224 | tf_op jit(solution)/shard_map/all_to_all | solution.py:199

commit v3 on v2

--- a/solution.py
+++ b/solution.py
@@ -10,15 +10,7 @@
 K1 = 8
 
 
-def edges(array, axis, dim, width):
-    peers, length = (lax.axis_size(axis), array.shape[dim])
-    up = [(i, (i + 1) % peers) for i in range(peers - 1)]
-    down = [(j, i) for i, j in up]
-    last = lax.slice_in_dim(array, length - width, length, axis=dim)
-    initial = lax.slice_in_dim(array, 0, width, axis=dim)
-    return [lax.ppermute(last, axis, up), array, lax.ppermute(initial, axis, down)]
-
-
+ANY = pl.BlockSpec(memory_space=pl.ANY)
 VM = pl.BlockSpec(memory_space=pltpu.VMEM)
 SM = pl.BlockSpec(memory_space=pltpu.SMEM)
 TOP = 14
@@ -67,20 +59,91 @@
     lax.fori_loop(0, upper_count, upper_step, 0, unroll=2)
 
 
+def halo_kernel(width_x, width_y, vec_ref, edge_ref, rows_ref, cols_ref, send_sem, recv_sem):
+    here_x = lax.axis_index("qx")
+    here_y = lax.axis_index("qy")
+    rows = vec_ref.shape[1]
+    leaf_x = edge_ref.shape[1]
+    steps = [(1, 0), (-1, 0), (0, 1), (0, -1), (1, 1), (1, -1), (-1, 1), (-1, -1)]
+
+    def present(dx, dy):
+        x = here_x + dx
+        y = here_y + dy
+        return (x >= 0) & (x < width_x) & (y >= 0) & (y < width_y)
+
+    def copy_of(n):
+        dx, dy = steps[n]
+        if dy == 0:
+            first = rows - LS if dx > 0 else 0
+            src = vec_ref.at[:, pl.ds(first, LS), :]
+            dst = rows_ref.at[0 if dx > 0 else 1]
+        else:
+            side = 1 if dy > 0 else 0
+            if dx == 0:
+                src = edge_ref.at[side]
+                dst = cols_ref.at[1 - side, pl.ds(1, leaf_x)]
+            else:
+                src = edge_ref.at[side, leaf_x - 1 if dx > 0 else 0]
+                dst = cols_ref.at[1 - side, 0 if dx > 0 else leaf_x + 1]
+        return pltpu.make_async_remote_copy(
+            src_ref=src,
+            dst_ref=dst,
+            send_sem=send_sem.at[n],
+            recv_sem=recv_sem.at[n],
+            device_id=(here_x + dx, here_y + dy),
+            device_id_type=pl.DeviceIdType.MESH,
+        )
+
+    barrier = pltpu.get_barrier_semaphore()
+    for dx, dy in steps:
+
+        @pl.when(present(dx, dy))
+        def _():
+            pl.semaphore_signal(
+                barrier,
+                inc=1,
+                device_id=(here_x + dx, here_y + dy),
+                device_id_type=pl.DeviceIdType.MESH,
+            )
+
+    spans = []
+    for here, width in ((here_x, width_x), (here_y, width_y)):
+        spans.append(1 + (here > 0).astype(jnp.int32) + (here < width - 1).astype(jnp.int32))
+    pl.semaphore_wait(barrier, spans[0] * spans[1] - 1)
+
+    for n, (dx, dy) in enumerate(steps):
+
+        @pl.when(present(dx, dy))
+        def _():
+            copy_of(n).start()
+
+    for n, (dx, dy) in enumerate(steps):
+
+        @pl.when(present(dx, dy))
+        def _():
+            copy_of(n).wait_send()
+
+        @pl.when(present(-dx, -dy))
+        def _():
+            copy_of(n).wait_recv()
+
+
 def near_kernel(leaf_y, off_ref, tiles_ref, grid_ref, out_ref):
-    m = pl.program_id(0)
-    i = m // leaf_y
-    j = lax.rem(m, leaf_y)
     vecs = grid_ref.shape[2]
-    total = None
-    for k in range(tiles_ref.shape[1]):
-        o = off_ref[m, k]
-        x = (i + o // 3) * LS
-        y = pl.multiple_of((j + lax.rem(o, 3)) * LS, LS)
-        block = grid_ref[pl.ds(x, LS), pl.ds(y, LS), :].reshape(LS * LS, vecs)
-        term = jnp.dot(tiles_ref[0, k], block, preferred_element_type=jnp.float32)
-        total = term if total is None else total + term
-    out_ref[0] = total
+    per = tiles_ref.shape[0]
+    for u in range(per):
+        m = pl.program_id(0) * per + u
+        i = m // leaf_y
+        j = lax.rem(m, leaf_y)
+        total = None
+        for k in range(tiles_ref.shape[1]):
+            o = off_ref[m, k]
+            x = (i + o // 3) * LS
+            y = pl.multiple_of((j + lax.rem(o, 3)) * LS, LS)
+            block = grid_ref[pl.ds(x, LS), pl.ds(y, LS), :].reshape(LS * LS, vecs)
+            term = jnp.dot(tiles_ref[u, k], block, preferred_element_type=jnp.float32)
+            total = term if total is None else total + term
+        out_ref[u] = total
 
 
 def far_kernel(leaf_x, leaf_y, tgt_ref, recv_ref, down_ref, row_ref, near_ref, out_ref, acc, full):
@@ -152,8 +215,9 @@
     fold = (rank_size // 2, 2 * vec_count)
     my_index = lax.axis_index("qx") * width_y + lax.axis_index("qy")
 
-    tall = jnp.concatenate(edges(vectors, "qx", 1, LS), axis=1)
-    pieces = edges(tall, "qy", 2, LS)
+    minor = vectors.transpose(1, 2, 0)
+    strips = jnp.stack([minor[:, :LS], minor[:, rows_y - LS :]]).reshape(2, leaf_x, LS, LS, vec_count)
+    strips = jnp.concatenate([strips[:, :, : LS // 2], strips[:, :, LS // 2 :]], axis=-1)
 
     blocks = (
         vectors.reshape(vec_count, leaf_x, LS, leaf_y, LS)
@@ -195,20 +259,49 @@
         ],
         axis=1,
     )
-    outgoing, pieces = lax.optimization_barrier((outgoing, pieces))
+    outgoing, strips = lax.optimization_barrier((outgoing, strips))
     arrived = lax.all_to_all(outgoing, ("qx", "qy"), split_axis=0, concat_axis=0, tiled=True)
 
-    grid = jnp.concatenate([piece.transpose(1, 2, 0) for piece in pieces], axis=1)
+    kind = vectors.dtype
+    near_rows, near_cols = pl.pallas_call(
+        lambda *refs: halo_kernel(width_x, width_y, *refs),
+        out_shape=(
+            shape((2, vec_count, LS, rows_y), kind),
+            shape((2, leaf_x + 2, LS // 2, LS, 2 * vec_count), kind),
+        ),
+        in_specs=[ANY, ANY],
+        out_specs=(ANY, ANY),
+        scratch_shapes=[pltpu.SemaphoreType.DMA((8,)), pltpu.SemaphoreType.DMA((8,))],
+        compiler_params=pltpu.CompilerParams(collective_id=0, has_side_effects=True),
+        cost_estimate=pl.CostEstimate(
+            flops=0, bytes_accessed=64 * vec_count * LS * rows_y * 2, transcendentals=0
+        ),
+        name="halo",
+    )(vectors, strips)
+    here_x = lax.axis_index("qx")
+    here_y = lax.axis_index("qy")
+    has_x = jnp.stack([here_x > 0, here_x < width_x - 1])
+    has_y = jnp.stack([here_y > 0, here_y < width_y - 1])
+    near_rows = jnp.where(has_x[:, None, None, None], near_rows, 0).transpose(0, 2, 3, 1)
+    tall = jnp.concatenate([near_rows[0], minor, near_rows[1]], axis=0)
+    along = jnp.concatenate([has_x[:1], jnp.ones((leaf_x,), bool), has_x[1:]])
+    valid = has_y[:, None] & along[None, :]
+    near_cols = jnp.where(valid[:, :, None, None, None], near_cols, 0)
+    near_cols = jnp.concatenate(
+        [near_cols[..., :vec_count], near_cols[..., vec_count:]], axis=2
+    ).reshape(2, rows_x + 2 * LS, LS, vec_count)
+    grid = jnp.concatenate([near_cols[0], tall, near_cols[1]], axis=1)
+    per = 4 if leaf_count % 4 == 0 else 1
     near = pl.pallas_call(
         lambda *refs: near_kernel(leaf_y, *refs),
-        grid=(leaf_count,),
+        grid=(leaf_count // per,),
         out_shape=shape((leaf_count, points, vec_count), f32),
         in_specs=[
             SM,
-            pl.BlockSpec((1, near_count, points, points), lambda m: (m, 0, 0, 0)),
+            pl.BlockSpec((per, near_count, points, points), lambda m: (m, 0, 0, 0)),
             VM,
         ],
-        out_specs=pl.BlockSpec((1, points, vec_count), lambda m: (m, 0, 0)),
+        out_specs=pl.BlockSpec((per, points, vec_count), lambda m: (m, 0, 0)),
         cost_estimate=pl.CostEstimate(
             flops=2 * leaf_count * near_count * points * points * vec_count,
             bytes_accessed=leaf_count * near_count * points * points * 2,

time: 89.1 us -> 90.4 us (1.015)
  the two profiles are of different devices: /device:TPU:0 before, /device:TPU:13 now
where the time goes in v3:
time: 90.4 us; the launch traced here: 89.9 us
  Pallas kernels  54.2 us (60%)
  local copies, waits for them, and re-layouts  14.1 us (16%)
  other arithmetic  13.7 us (15%)
  starting transfers between devices  6.27 us (7%)
  matrix products  1.4 us (2%)
    pallas_call x1, Pallas kernels, body(): pl.pallas_call(lambda *refs: halo_kernel(width_x, width_y, *refs), out_sh...  33.6 us
    unnamed x17, local copies, waits for them, and re-layouts  7.49 us
    pallas_call x1, Pallas kernels, body(): pl.pallas_call(lambda *refs: far_kernel(leaf_x, leaf_y, *refs), out_shape...  7.29 us
    pallas_call x1, Pallas kernels, body(): pl.pallas_call(lambda *refs: contrib_kernel(leaf_count, upper_count, *ref...  6.74 us
    pallas_call x1, Pallas kernels, body(): pl.pallas_call(lambda *refs: near_kernel(leaf_y, *refs), grid=(leaf_count...  6.61 us
    all_to_all x1, starting transfers between devices, body(): lax.all_to_all(outgoing, ('qx', 'qy'), split_axis=0, concat_axis=0, tiled...  6.27 us
    concatenate x1, other arithmetic, body(): grid = jnp.concatenate([near_cols[0], tall, near_cols[1]], axis=1)  3.69 us
    pallas_call x1, local copies, waits for them, and re-layouts, body(): pl.pallas_call(lambda *refs: halo_kernel(width_x, width_y, *refs), out_sh...  2.47 us
  transfers between devices with their start and end apart: 1, of which 0 were waited for; matrix products, arithmetic and copies ran while one was open for 11% of the time, Pallas kernels for 45%

profile of v3, /device:TPU:13, one launch (start us, length us, event | category | flops | bytes accessed | tf_op | source)
XLA Modules:
  0.0 89.9 jit_solution(5701590219133743581)
XLA Ops:
  0.0 0.7 dynamic-slice_bitcast_fusion
  0.9 1.2 %compare_select_fusion.refs_0_ = s32[128]{0:T(128)} fusion(s32[128]{0:T(128)S(1)} %convert_reduce_fusion, s32[32,128]{1,0:T(8,128)} %param.18, s32[]{:T(128)S(6)} %select_n.21), kind=kLoop, calls=%fused_computation.31 | loop fusion | flops 512 | bytes 1540 | tf_op jit(solution)/shard_map/jit(_where)/select_n | solution.py:237
  2.2 1.8 %copy.52 = bf16[64,32,128]{0,2,1:T(8,128)(2,1)S(1)} copy(bf16[64,32,128]{2,1,0:T(8,128)(2,1)} %refs_0_.1) | data formatting | bytes 1048576 | tf_op args[0]
  4.2 0.3 fusion.9
  4.5 1.1 %fusion.10 = f32[8,64,64,1]{2,1,0,3:T(8,128)S(1)} fusion(f32[2,8,64,64]{3,2,1,0:T(8,128)S(1)} %fusion.9, f32[2,8,64,64]{3,2,1,0:T(8,128)S(1)} %copy-done.3), kind=kOutput, calls=%fused_computation.42 | convolution fusion | flops 50331648 | bytes 655360 | tf_op jit(solution)/shard_map/ijrs,ijsv->ijrv/dot_general | solution.py:228
  5.7 0.8 copy.56.refs_3_
  6.4 5.6 %copy.51 = f32[1,128,64,64]{3,2,1,0:T(8,128)} copy(f32[1,128,64,64]{1,3,2,0:T(8,128)} %param.17) | data formatting | bytes 4194304 | tf_op args[7]
  12.0 6.7 %contrib.1 = (f32[129,32,128]{2,1,0:T(8,128)}, f32[129,128]{1,0:T(8,128)}) custom-call(s32[128]{0:T(128)} %compare_select_fusion.refs_0_, f32[128,64,64]{2,1,0:T(8,128)} %bitcast.43, f32[16,64,64]{2,1,0:T(8,128)} %bitcast.48, f32[4,64,64]{2,1,0:T(8,128)} %copy.56.refs_3_), custom_call_target="tpu_custom_call" | custom-call | flops 268435456 | bytes 33554432 | tf_op jit(solution)/shard_map/contrib/pallas_call | solution.py:238
  18.7 0.9 %slice_reduce_fusion = f32[128]{0:T(128)S(1)} fusion(f32[129,128]{1,0:T(8,128)} %get-tuple-element.12), kind=kLoop, calls=%fused_computation.17 | loop fusion | flops 16256 | bytes 66048 | tf_op jit(solution)/shard_map/reduce_max | solution.py:251
  19.9 0.8 fusion.2.refs_1_
  20.6 1.9 %multiply_convert_fusion = f16[128,32,128]{2,1,0:T(8,128)(2,1)S(1)} fusion(f32[129,32,128]{2,1,0:T(8,128)} %get-tuple-element.11, f32[128]{0:T(128)S(1)} %get-tuple-element.27), kind=kLoop, calls=%fused_computation.2 | loop fusion | flops 1048576 | bytes 3146240 | tf_op jit(solution)/shard_map/convert_element_type | solution.py:257
  22.6 1.3 %pad_maximum_fusion.1 = f16[32,132,128]{2,1,0:T(8,128)(2,1)} fusion(f16[32,4,128]{2,1,0:T(4,128)(2,1)S(1)} %broadcast_in_dim.61, f16[32,128,128]{2,1,0:T(8,128)(2,1)S(1)} %bitcast.49), kind=kLoop, calls=%fused_computation.3 | loop fusion | flops 540672 | bytes 2162688 | tf_op jit(solution)/shard_map/concatenate | solution.py:255
  24.0 6.3 %all-to-all-start = ((f16[32,132,128]{2,1,0:T(8,128)(2,1)}), f16[32,132,128]{2,1,0:T(8,128)(2,1)S(1)}, u32[]{:S(2)}, u32[]{:S(2)}) async-start(f16[32,132,128]{2,1,0:T(8,128)(2,1)} %pad_maximum_fusion.1), calls=%async_computation | async-start | bytes 2228224 | tf_op jit(solution)/shard_map/all_to_all | solution.py:263
  30.3 0.3 reduce_window_sum.11
  30.8 33.6 %halo.1 = (bf16[2,64,16,128]{3,2,1,0:T(8,128)(2,1)}, bf16[2,4,8,16,128]{4,3,2,1,0:T(8,128)(2,1)}) custom-call(bf16[64,32,128]{2,1,0:T(8,128)(2,1)} %refs_0_.1, bf16[2,2,8,16,128]{4,3,2,1,0:T(8,128)(2,1)} %fusion.2.refs_1_), custom_call_target="tpu_custom_call" | custom-call | bytes 16777216 | tf_op jit(solution)/shard_map/halo/pallas_call | solution.py:266
  64.4 2.5 %copy.60 = bf16[2,64,16,128]{1,3,2,0:T(8,128)(2,1)} copy(bf16[2,64,16,128]{3,2,1,0:T(8,128)(2,1)} %get-tuple-element.16) | data formatting | bytes 1048576 | tf_op jit(solution)/shard_map/halo/pallas_call | solution.py:266
  66.8 0.7 copy.64
  67.6 0.6 add.32.refs_0_
  68.6 1.0 %broadcast_select_fusion = bf16[2,4,8,16,128]{4,3,2,1,0:T(8,128)(2,1)S(1)} fusion(bf16[2,4,8,16,128]{4,3,2,1,0:T(8,128)(2,1)} %get-tuple-element.15, pred[2,4]{1,0:T(4,128)(4,1)S(1)} %broadcast_and_fusion), kind=kLoop, calls=%fused_computation.13 | loop fusion | flops 131072 | bytes 524296 | tf_op jit(solution)/shard_map/jit(_where)/select_n | solution.py:289
  70.1 3.7 %pad_maximum_fusion.refs_2_ = bf16[64,160,64]{2,1,0:T(8,128)(2,1)} fusion(bf16[64,16,64]{2,1,0:T(8,128)(2,1)S(1)} %bitcast.58, bf16[16,128,64]{2,1,0:T(8,128)(2,1)S(1)} %get-tuple-element.20, bf16[32,128,64]{2,1,0:T(8,128)(2,1)S(1)} %bitcast.46, bf16[16,128,64]{2,1,0:T(8,128)(2,1)S(1)} %get-tuple-element.19, bf16[64,16,64]{2,1,0:T(8,128)(2,1)S(1)} %bitcast.57), kind=kLoop, calls=%fused_computation | loop fusion | flops 6553600 | bytes 2621440 | tf_op jit(solution)/shard_map/concatenate | solution.py:293
  73.8 6.6 %near.1.refs_4_ = f32[16,256,64]{2,1,0:T(8,128)} custom-call(s32[16,3]{1,0:T(8,128)} %bitcast.61, bf16[16,3,256,256]{3,2,1,0:T(8,128)(2,1)} %bitcast.47, bf16[64,160,64]{2,1,0:T(8,128)(2,1)} %pad_maximum_fusion.refs_2_), custom_call_target="tpu_custom_call" | custom-call | flops 402653184 | bytes 6291456 | tf_op jit(solution)/shard_map/near/pallas_call | solution.py:295
  80.8 0.3 slice.62
  81.1 1.5 %convert_multiply_fusion.refs_1_ = f32[128,32,128]{2,1,0:T(8,128)} fusion(f16[128,32,128]{2,1,0:T(8,128)(2,1)S(1)} %bitcast.50, f32[128]{0:T(128)S(1)} %exp2.46), kind=kLoop, calls=%fused_computation.1 | loop fusion | flops 1048576 | bytes 3146240 | tf_op jit(solution)/shard_map/mul | solution.py:327
  82.6 7.3 %far.1 = f32[64,32,128]{2,1,0:T(8,128)} custom-call(s32[128]{0:T(128)} %add.32.refs_0_, f32[128,32,128]{2,1,0:T(8,128)} %convert_multiply_fusion.refs_1_, f32[16,64,64]{2,1,0:T(8,128)} %bitcast.59, bf16[16,64,256]{2,1,0:T(8,128)(2,1)} %bitcast.60, f32[16,256,64]{2,1,0:T(8,128)} %near.1.refs_4_), custom_call_target="tpu_custom_call" | custom-call | tf_op jit(solution)/shard_map/far/pallas_call | solution.py:328
  (42 shorter events, 2.2 us)
Async XLA Ops:
  0.0 4.2 %copy-start = (bf16[2,8,64,256]{3,2,1,0:T(8,128)(2,1)S(1)}, bf16[2,8,64,256]{3,2,1,0:T(8,128)(2,1)}, u32[]{:S(2)}) copy-start(bf16[2,8,64,256]{3,2,1,0:T(8,128)(2,1)} %param.13) | copy-start | bytes 1572868
  2.1 2.4 %copy-start.3 = (f32[2,8,64,64]{3,2,1,0:T(8,128)S(1)}, f32[2,8,64,64]{3,2,1,0:T(8,128)}, u32[]{:S(2)}) copy-start(f32[2,8,64,64]{3,2,1,0:T(8,128)} %param.15) | copy-start | bytes 786436
  4.5 7.5 %copy-start.1 = (f32[2,8,64,64]{3,2,1,0:T(8,128)}, f32[2,8,64,64]{3,2,1,0:T(8,128)S(1)}, u32[]{:S(2)}) copy-start(f32[2,8,64,64]{3,2,1,0:T(8,128)S(1)} %fusion.9) | copy-start | bytes 786436
  22.5 7.7 %copy-start.4 = (s32[32,128]{1,0:T(8,128)S(1)}, s32[32,128]{1,0:T(8,128)}, u32[]{:S(2)}) copy-start(s32[32,128]{1,0:T(8,128)} %param.18) | copy-start | bytes 49156
  22.5 8.0 %copy-start.5 = (s32[32,128]{1,0:T(8,128)S(1)}, s32[32,128]{1,0:T(8,128)}, u32[]{:S(2)}) copy-start(s32[32,128]{1,0:T(8,128)} %param.19) | copy-start | bytes 49156
  24.0 42.9 %copy-start.6 = (s32[2,8,3]{1,0,2:T(2,128)S(1)}, s32[2,8,3]{1,0,2:T(2,128)}, u32[]{:S(2)}) copy-start(s32[2,8,3]{1,0,2:T(2,128)} %param.12) | copy-start | bytes 580
  24.0 56.5 %all-to-all-start = ((f16[32,132,128]{2,1,0:T(8,128)(2,1)}), f16[32,132,128]{2,1,0:T(8,128)(2,1)S(1)}, u32[]{:S(2)}, u32[]{:S(2)}) async-start(f16[32,132,128]{2,1,0:T(8,128)(2,1)} %pad_maximum_fusion.1), calls=%async_computation | async-start | bytes 2228224 | tf_op jit(solution)/shard_map/all_to_all | solution.py:263
  68.2 1.6 %copy-start.2 = (bf16[2,64,16,128]{1,3,2,0:T(8,128)(2,1)S(1)}, bf16[2,64,16,128]{1,3,2,0:T(8,128)(2,1)}, u32[]{:S(2)}) copy-start(bf16[2,64,16,128]{1,3,2,0:T(8,128)(2,1)} %copy.60) | copy-start | bytes 1572868

commit v4 on v3

--- a/solution.py
+++ b/solution.py
@@ -31,21 +31,17 @@
     )
 
 
-def contrib_kernel(leaf_count, upper_count, pos_ref, coup_ref, leaf_ref, upper_ref, out_ref, max_ref):
+def contributions(leaf_count, upper_count, slot_ref, coup_ref, leaf_ref, upper_ref, out_ref, max_ref, held):
     rank = coup_ref.shape[1]
     half = rank // 2
-    out_ref[...] = jnp.zeros_like(out_ref)
-    max_ref[...] = jnp.zeros_like(max_ref)
+    held[held.shape[0] - 1] = jnp.zeros_like(held[0])
 
     def group(first, count, coef):
         mats = coup_ref[pl.ds(first, count)].reshape(count * rank, rank)
         res = product_of(mats, coef)
         for q in range(count):
-            row = pos_ref[first + q]
             one = res[q * rank : (q + 1) * rank]
-            folded = jnp.concatenate([one[:half], one[half:]], axis=1)
-            out_ref[row] = folded
-            max_ref[pl.ds(row, 1), :] = jnp.max(jnp.abs(folded), axis=0, keepdims=True)
+            held[first + q] = jnp.concatenate([one[:half], one[half:]], axis=1)
 
     def leaf_step(m, carry):
         group(m * K0, K0, leaf_ref[m])
@@ -55,11 +51,36 @@
         group(leaf_count * K0 + m * K1, K1, upper_ref[m])
         return carry
 
+    def place(p, carry):
+        value = held[slot_ref[p]]
+        out_ref[p] = value
+        max_ref[pl.ds(p, 1), :] = jnp.max(jnp.abs(value), axis=0, keepdims=True)
+        return carry
+
     lax.fori_loop(0, leaf_count, leaf_step, 0, unroll=4)
     lax.fori_loop(0, upper_count, upper_step, 0, unroll=2)
-
-
-def halo_kernel(width_x, width_y, vec_ref, edge_ref, rows_ref, cols_ref, send_sem, recv_sem):
+    lax.fori_loop(0, out_ref.shape[0], place, 0, unroll=4)
+
+
+def first_kernel(
+    leaf_count,
+    upper_count,
+    width_x,
+    width_y,
+    slot_ref,
+    coup_ref,
+    leaf_ref,
+    upper_ref,
+    vec_ref,
+    edge_ref,
+    out_ref,
+    max_ref,
+    rows_ref,
+    cols_ref,
+    held,
+    send_sem,
+    recv_sem,
+):
     here_x = lax.axis_index("qx")
     here_y = lax.axis_index("qy")
     rows = vec_ref.shape[1]
@@ -116,6 +137,10 @@
         @pl.when(present(dx, dy))
         def _():
             copy_of(n).start()
+
+    contributions(
+        leaf_count, upper_count, slot_ref, coup_ref, leaf_ref, upper_ref, out_ref, max_ref, held
+    )
 
     for n, (dx, dy) in enumerate(steps):
 
@@ -235,22 +260,38 @@
     order_in = jnp.sum((same_dest & earlier).astype(jnp.int32), axis=1)
     spare_row = devices * capacity
     position = jnp.where(own_dest >= 0, own_dest * capacity + order_in, spare_row)
-    placed, peaks = pl.pallas_call(
-        lambda *refs: contrib_kernel(leaf_count, upper_count, *refs),
-        out_shape=(shape((spare_row + 1,) + fold, f32), shape((spare_row + 1, fold[1]), f32)),
-        in_specs=[SM, VM, VM, VM],
-        out_specs=(VM, VM),
-        cost_estimate=pl.CostEstimate(
-            flops=8 * slot_count * rank_size * rank_size * vec_count,
-            bytes_accessed=16 * slot_count * rank_size * rank_size * 4,
-            transcendentals=0,
+    filled = position[None, :] == jnp.arange(spare_row, dtype=jnp.int32)[:, None]
+    slot_of = slot_count + jnp.sum(jnp.where(filled, slot_ident - slot_count, 0), axis=1)
+    kind = vectors.dtype
+    placed, peaks, near_rows, near_cols = pl.pallas_call(
+        lambda *refs: first_kernel(leaf_count, upper_count, width_x, width_y, *refs),
+        out_shape=(
+            shape((spare_row,) + fold, f32),
+            shape((spare_row, fold[1]), f32),
+            shape((2, vec_count, LS, rows_y), kind),
+            shape((2, leaf_x + 2, LS // 2, LS, 2 * vec_count), kind),
         ),
+        in_specs=[SM, VM, VM, VM, ANY, ANY],
+        out_specs=(VM, VM, ANY, ANY),
+        scratch_shapes=[
+            pltpu.VMEM((slot_count + 1,) + fold, f32),
+            pltpu.SemaphoreType.DMA((8,)),
+            pltpu.SemaphoreType.DMA((8,)),
+        ],
+        compiler_params=pltpu.CompilerParams(collective_id=0, has_side_effects=True),
         name="contrib",
-    )(position, coupling[0], leaf_coef.reshape(leaf_count, rank_size, vec_count), upper_coef)
-
-    peak = jnp.max(peaks[:spare_row], axis=1)
+    )(
+        slot_of,
+        coupling[0],
+        leaf_coef.reshape(leaf_count, rank_size, vec_count),
+        upper_coef,
+        vectors,
+        strips,
+    )
+
+    peak = jnp.max(peaks, axis=1)
     power = jnp.ceil(jnp.log2(jnp.maximum(peak, 1e-30)))
-    scaled = placed[:spare_row] * jnp.exp2(TOP - power)[:, None, None]
+    scaled = placed * jnp.exp2(TOP - power)[:, None, None]
     notes = jnp.broadcast_to(power.reshape(devices, capacity, 1), (devices, capacity, fold[1]))
     outgoing = jnp.concatenate(
         [
@@ -259,25 +300,9 @@
         ],
         axis=1,
     )
-    outgoing, strips = lax.optimization_barrier((outgoing, strips))
+    outgoing, near_rows, near_cols = lax.optimization_barrier((outgoing, near_rows, near_cols))
     arrived = lax.all_to_all(outgoing, ("qx", "qy"), split_axis=0, concat_axis=0, tiled=True)
 
-    kind = vectors.dtype
-    near_rows, near_cols = pl.pallas_call(
-        lambda *refs: halo_kernel(width_x, width_y, *refs),
-        out_shape=(
-            shape((2, vec_count, LS, rows_y), kind),
-            shape((2, leaf_x + 2, LS // 2, LS, 2 * vec_count), kind),
-        ),
-        in_specs=[ANY, ANY],
-        out_specs=(ANY, ANY),
-        scratch_shapes=[pltpu.SemaphoreType.DMA((8,)), pltpu.SemaphoreType.DMA((8,))],
-        compiler_params=pltpu.CompilerParams(collective_id=0, has_side_effects=True),
-        cost_estimate=pl.CostEstimate(
-            flops=0, bytes_accessed=64 * vec_count * LS * rows_y * 2, transcendentals=0
-        ),
-        name="halo",
-    )(vectors, strips)
     here_x = lax.axis_index("qx")
     here_y = lax.axis_index("qy")
     has_x = jnp.stack([here_x > 0, here_x < width_x - 1])

time: 90.4 us -> 81.7 us (0.904)
  the two profiles are of different devices: /device:TPU:13 before, /device:TPU:0 now
where the time goes in v4:
time: 81.7 us; the launch traced here: 81.2 us
  Pallas kernels  35.1 us (43%)
  local copies, waits for them, and re-layouts  13.6 us (17%)
  other arithmetic  12.9 us (16%)
  waiting for transfers between devices  12.5 us (15%)
  starting transfers between devices  5.55 us (7%)
  matrix products  1.4 us (2%)
    pallas_call x1, Pallas kernels, body(): pl.pallas_call(lambda *refs: first_kernel(leaf_count, upper_count, width_...  21.2 us
    all_to_all x1, waiting for transfers between devices, body(): lax.all_to_all(outgoing, ('qx', 'qy'), split_axis=0, concat_axis=0, tiled...  12.5 us
    unnamed x21, local copies, waits for them, and re-layouts  7.99 us
    pallas_call x1, Pallas kernels, body(): pl.pallas_call(lambda *refs: far_kernel(leaf_x, leaf_y, *refs), out_shape...  7.29 us
    pallas_call x1, Pallas kernels, body(): pl.pallas_call(lambda *refs: near_kernel(leaf_y, *refs), grid=(leaf_count...  6.61 us
    all_to_all x1, starting transfers between devices, body(): lax.all_to_all(outgoing, ('qx', 'qy'), split_axis=0, concat_axis=0, tiled...  5.55 us
    concatenate x1, other arithmetic, body(): grid = jnp.concatenate([near_cols[0], tall, near_cols[1]], axis=1)  3.71 us
    convert_element_type x1, other arithmetic, body(): scaled.reshape(devices, capacity * fold[0], fold[1]).astype(jnp.float16)  1.87 us
  transfers between devices with their start and end apart: 1, of which 1 were waited for; matrix products, arithmetic and copies ran while one was open for 10% of the time, Pallas kernels for 8%

profile of v4, /device:TPU:0, one launch (start us, length us, event | category | flops | bytes accessed | tf_op | source)
XLA Modules:
  0.0 81.2 jit_solution(2098763294198160857)
XLA Ops:
  0.0 0.7 fusion.6
  0.9 0.7 fusion.5
  1.7 0.5 broadcast_add_fusion.2.refs_0_
  2.3 1.7 %copy.52 = bf16[64,32,128]{0,2,1:T(8,128)(2,1)S(1)} copy(bf16[64,32,128]{2,1,0:T(8,128)(2,1)} %refs_4_.1) | data formatting | bytes 1048576 | tf_op args[0]
  4.1 0.8 fusion.2.refs_5_
  5.1 0.3 fusion.11
  5.4 1.1 %fusion.12 = f32[8,64,64,1]{2,1,0,3:T(8,128)S(1)} fusion(f32[2,8,64,64]{3,2,1,0:T(8,128)S(1)} %fusion.11, f32[2,8,64,64]{3,2,1,0:T(8,128)S(1)} %copy-done.4), kind=kOutput, calls=%fused_computation.48 | convolution fusion | flops 50331648 | bytes 655360 | tf_op jit(solution)/shard_map/ijrs,ijsv->ijrv/dot_general | solution.py:253
  6.6 0.8 copy.57.refs_3_
  7.3 5.6 %copy.51 = f32[1,128,64,64]{3,2,1,0:T(8,128)} copy(f32[1,128,64,64]{1,3,2,0:T(8,128)} %param.17) | data formatting | bytes 4194304 | tf_op args[7]
  12.9 21.2 %contrib.1 = (f32[128,32,128]{2,1,0:T(8,128)}, f32[128,128]{1,0:T(8,128)}, bf16[2,64,16,128]{3,2,1,0:T(8,128)(2,1)}, bf16[2,4,8,16,128]{4,3,2,1,0:T(8,128)(2,1)}) custom-call(s32[128]{0:T(128)} %broadcast_add_fusion.2.refs_0_, f32[128,64,64]{2,1,0:T(8,128)} %bitcast.47, f32[16,64,64]{2,1,0:T(8,128)} %bitcast.52, f32[4,64,64]{2,1,0:T(8,128)} %copy.57.refs_3_, ...), custom_call_target="tpu_custom_call" | custom-call | tf_op jit(solution)/shard_map/contrib/pallas_call | solution.py:266
  34.1 0.9 %reduce_max.9 = f32[128]{0:T(128)S(1)} reduce(f32[128,128]{1,0:T(8,128)} %get-tuple-element.13, f32[]{:T(128)} %constant.19.clone.1), dimensions={1}, to_apply=%region_5.6 | reduce | flops 16256 | bytes 66052 | tf_op jit(solution)/shard_map/reduce_max | solution.py:292
  35.2 1.9 %multiply_convert_fusion = f16[128,32,128]{2,1,0:T(8,128)(2,1)S(1)} fusion(f32[128,32,128]{2,1,0:T(8,128)} %get-tuple-element.12, f32[128]{0:T(128)S(1)} %get-tuple-element.29), kind=kLoop, calls=%fused_computation.2 | loop fusion | flops 1048576 | bytes 3146240 | tf_op jit(solution)/shard_map/convert_element_type | solution.py:298
  37.2 1.3 %pad_maximum_fusion.1 = f16[32,132,128]{2,1,0:T(8,128)(2,1)} fusion(f16[32,4,128]{2,1,0:T(4,128)(2,1)S(1)} %broadcast_in_dim.76, f16[32,128,128]{2,1,0:T(8,128)(2,1)S(1)} %bitcast.53), kind=kLoop, calls=%fused_computation.3 | loop fusion | flops 540672 | bytes 2162688 | tf_op jit(solution)/shard_map/concatenate | solution.py:296
  38.6 5.5 %all-to-all-start = ((f16[32,132,128]{2,1,0:T(8,128)(2,1)}), f16[32,132,128]{2,1,0:T(8,128)(2,1)S(1)}, u32[]{:S(2)}, u32[]{:S(2)}) async-start(f16[32,132,128]{2,1,0:T(8,128)(2,1)} %pad_maximum_fusion.1), calls=%async_computation | async-start | bytes 2228224 | tf_op jit(solution)/shard_map/all_to_all | solution.py:304
  44.2 0.3 reduce_window_sum.11
  44.6 1.5 %copy.60 = bf16[2,64,16,128]{1,3,2,0:T(8,128)(2,1)} copy(bf16[2,64,16,128]{3,2,1,0:T(8,128)(2,1)S(1)} %copy-done.3) | data formatting | bytes 1048576 | tf_op jit(solution)/shard_map/optimization_barrier | solution.py:303
  46.1 0.7 copy.64
  46.9 0.6 add.37.refs_0_
  48.2 0.5 copy-done.2
  49.0 3.7 %pad_maximum_fusion.refs_2_ = bf16[64,160,64]{2,1,0:T(8,128)(2,1)} fusion(bf16[64,16,64]{2,1,0:T(8,128)(2,1)S(1)} %bitcast.62, bf16[16,128,64]{2,1,0:T(8,128)(2,1)S(1)} %get-tuple-element.22, bf16[32,128,64]{2,1,0:T(8,128)(2,1)S(1)} %bitcast.50, bf16[16,128,64]{2,1,0:T(8,128)(2,1)S(1)} %get-tuple-element.21, bf16[64,16,64]{2,1,0:T(8,128)(2,1)S(1)} %bitcast.61), kind=kLoop, calls=%fused_computation | loop fusion | flops 6553600 | bytes 2621440 | tf_op jit(solution)/shard_map/concatenate | solution.py:318
  52.7 6.6 %near.1.refs_4_ = f32[16,256,64]{2,1,0:T(8,128)} custom-call(s32[16,3]{1,0:T(8,128)} %bitcast.65, bf16[16,3,256,256]{3,2,1,0:T(8,128)(2,1)} %bitcast.51, bf16[64,160,64]{2,1,0:T(8,128)(2,1)} %pad_maximum_fusion.refs_2_), custom_call_target="tpu_custom_call" | custom-call | flops 402653184 | bytes 6291456 | tf_op jit(solution)/shard_map/near/pallas_call | solution.py:320
  59.3 12.5 %all-to-all-done = f16[32,132,128]{2,1,0:T(8,128)(2,1)S(1)} async-done(((f16[32,132,128]{2,1,0:T(8,128)(2,1)}), f16[32,132,128]{2,1,0:T(8,128)(2,1)S(1)}, u32[]{:S(2)}, u32[]{:S(2)}) %all-to-all-start) | async-done | bytes 1081376 | tf_op jit(solution)/shard_map/all_to_all | solution.py:304
  72.4 1.6 %convert_multiply_fusion.refs_1_ = f32[128,32,128]{2,1,0:T(8,128)} fusion(f16[128,32,128]{2,1,0:T(8,128)(2,1)S(1)} %bitcast.54, f32[128]{0:T(128)S(1)} %exp2.46), kind=kLoop, calls=%fused_computation.1 | loop fusion | flops 1048576 | bytes 3146240 | tf_op jit(solution)/shard_map/mul | solution.py:352
  73.9 7.3 %far.1 = f32[64,32,128]{2,1,0:T(8,128)} custom-call(s32[128]{0:T(128)} %add.37.refs_0_, f32[128,32,128]{2,1,0:T(8,128)} %convert_multiply_fusion.refs_1_, f32[16,64,64]{2,1,0:T(8,128)} %bitcast.63, bf16[16,64,256]{2,1,0:T(8,128)(2,1)} %bitcast.64, f32[16,256,64]{2,1,0:T(8,128)} %near.1.refs_4_), custom_call_target="tpu_custom_call" | custom-call | tf_op jit(solution)/shard_map/far/pallas_call | solution.py:353
  (48 shorter events, 2.6 us)
Async XLA Ops:
  0.0 5.1 %copy-start = (bf16[2,8,64,256]{3,2,1,0:T(8,128)(2,1)S(1)}, bf16[2,8,64,256]{3,2,1,0:T(8,128)(2,1)}, u32[]{:S(2)}) copy-start(bf16[2,8,64,256]{3,2,1,0:T(8,128)(2,1)} %param.13) | copy-start | bytes 1572868
  4.0 1.4 %copy-start.4 = (f32[2,8,64,64]{3,2,1,0:T(8,128)S(1)}, f32[2,8,64,64]{3,2,1,0:T(8,128)}, u32[]{:S(2)}) copy-start(f32[2,8,64,64]{3,2,1,0:T(8,128)} %param.15) | copy-start | bytes 786436
  5.4 7.5 %copy-start.1 = (f32[2,8,64,64]{3,2,1,0:T(8,128)}, f32[2,8,64,64]{3,2,1,0:T(8,128)S(1)}, u32[]{:S(2)}) copy-start(f32[2,8,64,64]{3,2,1,0:T(8,128)S(1)} %fusion.11) | copy-start | bytes 786436
  37.1 7.1 %copy-start.6 = (s32[32,128]{1,0:T(8,128)S(1)}, s32[32,128]{1,0:T(8,128)}, u32[]{:S(2)}) copy-start(s32[32,128]{1,0:T(8,128)} %param.18) | copy-start | bytes 49156
  37.1 7.4 %copy-start.7 = (s32[32,128]{1,0:T(8,128)S(1)}, s32[32,128]{1,0:T(8,128)}, u32[]{:S(2)}) copy-start(s32[32,128]{1,0:T(8,128)} %param.19) | copy-start | bytes 49156
  37.1 7.5 %copy-start.3 = (bf16[2,64,16,128]{3,2,1,0:T(8,128)(2,1)S(1)}, bf16[2,64,16,128]{3,2,1,0:T(8,128)(2,1)}, u32[]{:S(2)}) copy-start(bf16[2,64,16,128]{3,2,1,0:T(8,128)(2,1)} %get-tuple-element.18) | copy-start | bytes 1572868
  37.2 8.9 %copy-start.8 = (s32[2,8,3]{1,0,2:T(2,128)S(1)}, s32[2,8,3]{1,0,2:T(2,128)}, u32[]{:S(2)}) copy-start(s32[2,8,3]{1,0,2:T(2,128)} %param.12) | copy-start | bytes 580
  37.2 10.6 %copy-start.5 = (bf16[2,4,8,16,128]{4,3,2,1,0:T(8,128)(2,1)S(1)}, bf16[2,4,8,16,128]{4,3,2,1,0:T(8,128)(2,1)}, u32[]{:S(2)}) copy-start(bf16[2,4,8,16,128]{4,3,2,1,0:T(8,128)(2,1)} %get-tuple-element.17) | copy-start | bytes 786436
  38.6 33.2 %all-to-all-start = ((f16[32,132,128]{2,1,0:T(8,128)(2,1)}), f16[32,132,128]{2,1,0:T(8,128)(2,1)S(1)}, u32[]{:S(2)}, u32[]{:S(2)}) async-start(f16[32,132,128]{2,1,0:T(8,128)(2,1)} %pad_maximum_fusion.1), calls=%async_computation | async-start | bytes 2228224 | tf_op jit(solution)/shard_map/all_to_all | solution.py:304
  47.5 1.2 %copy-start.2 = (bf16[2,64,16,128]{1,3,2,0:T(8,128)(2,1)S(1)}, bf16[2,64,16,128]{1,3,2,0:T(8,128)(2,1)}, u32[]{:S(2)}) copy-start(bf16[2,64,16,128]{1,3,2,0:T(8,128)(2,1)} %copy.60) | copy-start | bytes 1572868

commit v5 on v4

--- a/solution.py
+++ b/solution.py
@@ -31,13 +31,13 @@
     )
 
 
-def contributions(leaf_count, upper_count, slot_ref, coup_ref, leaf_ref, upper_ref, out_ref, max_ref, held):
+def contributions(leaf_count, upper_count, slot_ref, coup_ref, leaf_ref, upper_ref, out_ref, max_ref, mats_ref, held):
     rank = coup_ref.shape[1]
     half = rank // 2
     held[held.shape[0] - 1] = jnp.zeros_like(held[0])
 
     def group(first, count, coef):
-        mats = coup_ref[pl.ds(first, count)].reshape(count * rank, rank)
+        mats = mats_ref[pl.ds(first, count)].reshape(count * rank, rank)
         res = product_of(mats, coef)
         for q in range(count):
             one = res[q * rank : (q + 1) * rank]
@@ -57,6 +57,11 @@
         max_ref[pl.ds(p, 1), :] = jnp.max(jnp.abs(value), axis=0, keepdims=True)
         return carry
 
+    def turn(r, carry):
+        mats_ref[:, r, :] = coup_ref[r].T
+        return carry
+
+    lax.fori_loop(0, rank, turn, 0, unroll=4)
     lax.fori_loop(0, leaf_count, leaf_step, 0, unroll=4)
     lax.fori_loop(0, upper_count, upper_step, 0, unroll=2)
     lax.fori_loop(0, out_ref.shape[0], place, 0, unroll=4)
@@ -77,6 +82,7 @@
     max_ref,
     rows_ref,
     cols_ref,
+    mats_ref,
     held,
     send_sem,
     recv_sem,
@@ -139,7 +145,7 @@
             copy_of(n).start()
 
     contributions(
-        leaf_count, upper_count, slot_ref, coup_ref, leaf_ref, upper_ref, out_ref, max_ref, held
+        leaf_count, upper_count, slot_ref, coup_ref, leaf_ref, upper_ref, out_ref, max_ref, mats_ref, held
     )
 
     for n, (dx, dy) in enumerate(steps):
@@ -274,6 +280,7 @@
         in_specs=[SM, VM, VM, VM, ANY, ANY],
         out_specs=(VM, VM, ANY, ANY),
         scratch_shapes=[
+            pltpu.VMEM((slot_count, rank_size, rank_size), f32),
             pltpu.VMEM((slot_count + 1,) + fold, f32),
             pltpu.SemaphoreType.DMA((8,)),
             pltpu.SemaphoreType.DMA((8,)),
@@ -282,7 +289,7 @@
         name="contrib",
     )(
         slot_of,
-        coupling[0],
+        coupling[0].transpose(1, 2, 0),
         leaf_coef.reshape(leaf_count, rank_size, vec_count),
         upper_coef,
         vectors,

time: 81.7 us -> 75.6 us (0.925)
  local copies, waits for them, and re-layouts: 13.6 us -> 7.99 us
    unnamed x21 -> x20, local copies, waits for them, and re-layouts: 7.99 us -> 2.42 us
  transfers between devices with their start and end apart: 1 -> 1, of which waited for: 1 -> 1; matrix products, arithmetic and copies ran while one was open for 10% -> 11% of each run, Pallas kernels for 8% -> 9%
where the time goes in v5:
time: 75.6 us; the launch traced here: 75.2 us
  Pallas kernels  34.5 us (46%)
  other arithmetic  12.9 us (17%)
  waiting for transfers between devices  12.5 us (17%)
  local copies, waits for them, and re-layouts  7.99 us (11%)
  starting transfers between devices  5.55 us (7%)
  matrix products  1.4 us (2%)
    pallas_call x1, Pallas kernels, body(): pl.pallas_call(lambda *refs: first_kernel(leaf_count, upper_count, width_...  20.6 us
    all_to_all x1, waiting for transfers between devices, body(): lax.all_to_all(outgoing, ('qx', 'qy'), split_axis=0, concat_axis=0, tiled...  12.5 us
    pallas_call x1, Pallas kernels, body(): pl.pallas_call(lambda *refs: far_kernel(leaf_x, leaf_y, *refs), out_shape...  7.29 us
    pallas_call x1, Pallas kernels, body(): pl.pallas_call(lambda *refs: near_kernel(leaf_y, *refs), grid=(leaf_count...  6.6 us
    all_to_all x1, starting transfers between devices, body(): lax.all_to_all(outgoing, ('qx', 'qy'), split_axis=0, concat_axis=0, tiled...  5.55 us
    concatenate x1, other arithmetic, body(): grid = jnp.concatenate([near_cols[0], tall, near_cols[1]], axis=1)  3.71 us
    unnamed x20, local copies, waits for them, and re-layouts  2.42 us
    convert_element_type x1, other arithmetic, body(): scaled.reshape(devices, capacity * fold[0], fold[1]).astype(jnp.float16)  1.87 us
  transfers between devices with their start and end apart: 1, of which 1 were waited for; matrix products, arithmetic and copies ran while one was open for 11% of the time, Pallas kernels for 9%

profile of v5, /device:TPU:0, one launch (start us, length us, event | category | flops | bytes accessed | tf_op | source)
XLA Modules:
  0.0 75.2 jit_solution(885914404108484808)
XLA Ops:
  0.0 0.7 fusion.6
  0.9 0.7 fusion.5
  1.7 0.6 broadcast_add_fusion.2.refs_0_
  2.3 1.7 %copy.47 = bf16[64,32,128]{0,2,1:T(8,128)(2,1)S(1)} copy(bf16[64,32,128]{2,1,0:T(8,128)(2,1)} %refs_4_.1) | data formatting | bytes 1048576 | tf_op args[0]
  4.1 0.8 %fusion.2.refs_5_ = bf16[2,2,8,16,128]{4,3,2,1,0:T(8,128)(2,1)} fusion(bf16[1,2,16,16,64]{4,3,2,1,0:T(8,128)(2,1)S(1)} %bitcast.61, bf16[1,2,16,16,64]{4,3,2,1,0:T(8,128)(2,1)S(1)} %bitcast.59, bf16[2,2,8,16,64]{4,3,2,1,0:T(8,128)(2,1)S(1)} %fusion.1), kind=kLoop, calls=%fused_computation.16 | loop fusion | flops 393216 | bytes 327680 | tf_op jit(solution)/shard_map/concatenate | solution.py:251
  5.2 0.3 fusion.11
  5.5 1.1 %fusion.12 = f32[8,64,64,1]{2,1,0,3:T(8,128)S(1)} fusion(f32[2,8,64,64]{3,2,1,0:T(8,128)S(1)} %fusion.11, f32[2,8,64,64]{3,2,1,0:T(8,128)S(1)} %copy-done.4), kind=kOutput, calls=%fused_computation.48 | convolution fusion | flops 50331648 | bytes 655360 | tf_op jit(solution)/shard_map/ijrs,ijsv->ijrv/dot_general | solution.py:259
  6.6 0.8 %copy.52.refs_3_ = f32[4,64,64]{2,1,0:T(8,128)} copy(f32[4,64,64]{1,2,0:T(8,128)S(1)} %reduce_sum.48) | data formatting | bytes 131072 | tf_op jit(solution)/shard_map/reduce_sum | solution.py:260
  7.4 20.6 %contrib.1 = (f32[128,32,128]{2,1,0:T(8,128)}, f32[128,128]{1,0:T(8,128)}, bf16[2,64,16,128]{3,2,1,0:T(8,128)(2,1)}, bf16[2,4,8,16,128]{4,3,2,1,0:T(8,128)(2,1)}) custom-call(s32[128]{0:T(128)} %broadcast_add_fusion.2.refs_0_, f32[64,64,128]{2,1,0:T(8,128)} %bitcast.57, f32[16,64,64]{2,1,0:T(8,128)} %bitcast.53, f32[4,64,64]{2,1,0:T(8,128)} %copy.52.refs_3_, ...), custom_call_target="tpu_custom_call" | custom-call | tf_op jit(solution)/shard_map/contrib/pallas_call | solution.py:272
  28.0 0.9 %reduce_max.9 = f32[128]{0:T(128)S(1)} reduce(f32[128,128]{1,0:T(8,128)} %get-tuple-element.13, f32[]{:T(128)} %constant.19.clone.1), dimensions={1}, to_apply=%region_5.6 | reduce | flops 16256 | bytes 66052 | tf_op jit(solution)/shard_map/reduce_max | solution.py:299
  29.1 1.9 %multiply_convert_fusion = f16[128,32,128]{2,1,0:T(8,128)(2,1)S(1)} fusion(f32[128,32,128]{2,1,0:T(8,128)} %get-tuple-element.12, f32[128]{0:T(128)S(1)} %get-tuple-element.29), kind=kLoop, calls=%fused_computation.2 | loop fusion | flops 1048576 | bytes 3146240 | tf_op jit(solution)/shard_map/convert_element_type | solution.py:305
  31.2 1.3 %pad_maximum_fusion.1 = f16[32,132,128]{2,1,0:T(8,128)(2,1)} fusion(f16[32,4,128]{2,1,0:T(4,128)(2,1)S(1)} %broadcast_in_dim.76, f16[32,128,128]{2,1,0:T(8,128)(2,1)S(1)} %bitcast.54), kind=kLoop, calls=%fused_computation.3 | loop fusion | flops 540672 | bytes 2162688 | tf_op jit(solution)/shard_map/concatenate | solution.py:303
  32.5 5.6 %all-to-all-start = ((f16[32,132,128]{2,1,0:T(8,128)(2,1)}), f16[32,132,128]{2,1,0:T(8,128)(2,1)S(1)}, u32[]{:S(2)}, u32[]{:S(2)}) async-start(f16[32,132,128]{2,1,0:T(8,128)(2,1)} %pad_maximum_fusion.1), calls=%async_computation | async-start | bytes 2228224 | tf_op jit(solution)/shard_map/all_to_all | solution.py:311
  38.1 0.3 reduce_window_sum.11
  38.6 1.5 %copy.55 = bf16[2,64,16,128]{1,3,2,0:T(8,128)(2,1)} copy(bf16[2,64,16,128]{3,2,1,0:T(8,128)(2,1)S(1)} %copy-done.3) | data formatting | bytes 1048576 | tf_op jit(solution)/shard_map/optimization_barrier | solution.py:310
  40.0 0.7 copy.59
  40.8 0.6 add.37.refs_0_
  42.1 0.5 copy-done.2
  42.9 3.7 %pad_maximum_fusion.refs_2_ = bf16[64,160,64]{2,1,0:T(8,128)(2,1)} fusion(bf16[64,16,64]{2,1,0:T(8,128)(2,1)S(1)} %bitcast.64, bf16[16,128,64]{2,1,0:T(8,128)(2,1)S(1)} %get-tuple-element.22, bf16[32,128,64]{2,1,0:T(8,128)(2,1)S(1)} %bitcast.51, bf16[16,128,64]{2,1,0:T(8,128)(2,1)S(1)} %get-tuple-element.21, bf16[64,16,64]{2,1,0:T(8,128)(2,1)S(1)} %bitcast.63), kind=kLoop, calls=%fused_computation | loop fusion | flops 6553600 | bytes 2621440 | tf_op jit(solution)/shard_map/concatenate | solution.py:325
  46.6 6.6 %near.1.refs_4_ = f32[16,256,64]{2,1,0:T(8,128)} custom-call(s32[16,3]{1,0:T(8,128)} %bitcast.67, bf16[16,3,256,256]{3,2,1,0:T(8,128)(2,1)} %bitcast.52, bf16[64,160,64]{2,1,0:T(8,128)(2,1)} %pad_maximum_fusion.refs_2_), custom_call_target="tpu_custom_call" | custom-call | flops 402653184 | bytes 6291456 | tf_op jit(solution)/shard_map/near/pallas_call | solution.py:327
  53.2 12.5 %all-to-all-done = f16[32,132,128]{2,1,0:T(8,128)(2,1)S(1)} async-done(((f16[32,132,128]{2,1,0:T(8,128)(2,1)}), f16[32,132,128]{2,1,0:T(8,128)(2,1)S(1)}, u32[]{:S(2)}, u32[]{:S(2)}) %all-to-all-start) | async-done | bytes 1081376 | tf_op jit(solution)/shard_map/all_to_all | solution.py:311
  66.0 0.3 slice.54
  66.3 1.6 %convert_multiply_fusion.refs_1_ = f32[128,32,128]{2,1,0:T(8,128)} fusion(f16[128,32,128]{2,1,0:T(8,128)(2,1)S(1)} %bitcast.55, f32[128]{0:T(128)S(1)} %exp2.46), kind=kLoop, calls=%fused_computation.1 | loop fusion | flops 1048576 | bytes 3146240 | tf_op jit(solution)/shard_map/mul | solution.py:359
  67.9 7.3 %far.1 = f32[64,32,128]{2,1,0:T(8,128)} custom-call(s32[128]{0:T(128)} %add.37.refs_0_, f32[128,32,128]{2,1,0:T(8,128)} %convert_multiply_fusion.refs_1_, f32[16,64,64]{2,1,0:T(8,128)} %bitcast.65, bf16[16,64,256]{2,1,0:T(8,128)(2,1)} %bitcast.66, f32[16,256,64]{2,1,0:T(8,128)} %near.1.refs_4_), custom_call_target="tpu_custom_call" | custom-call | tf_op jit(solution)/shard_map/far/pallas_call | solution.py:360
  (47 shorter events, 2.4 us)
Async XLA Ops:
  0.0 5.2 %copy-start = (bf16[2,8,64,256]{3,2,1,0:T(8,128)(2,1)S(1)}, bf16[2,8,64,256]{3,2,1,0:T(8,128)(2,1)}, u32[]{:S(2)}) copy-start(bf16[2,8,64,256]{3,2,1,0:T(8,128)(2,1)} %param.13) | copy-start | bytes 1572868
  4.1 1.4 %copy-start.4 = (f32[2,8,64,64]{3,2,1,0:T(8,128)S(1)}, f32[2,8,64,64]{3,2,1,0:T(8,128)}, u32[]{:S(2)}) copy-start(f32[2,8,64,64]{3,2,1,0:T(8,128)} %param.15) | copy-start | bytes 786436
  5.5 1.9 %copy-start.1 = (f32[2,8,64,64]{3,2,1,0:T(8,128)}, f32[2,8,64,64]{3,2,1,0:T(8,128)S(1)}, u32[]{:S(2)}) copy-start(f32[2,8,64,64]{3,2,1,0:T(8,128)S(1)} %fusion.11) | copy-start | bytes 786436
  31.0 7.1 %copy-start.6 = (s32[32,128]{1,0:T(8,128)S(1)}, s32[32,128]{1,0:T(8,128)}, u32[]{:S(2)}) copy-start(s32[32,128]{1,0:T(8,128)} %param.18) | copy-start | bytes 49156
  31.0 7.4 %copy-start.7 = (s32[32,128]{1,0:T(8,128)S(1)}, s32[32,128]{1,0:T(8,128)}, u32[]{:S(2)}) copy-start(s32[32,128]{1,0:T(8,128)} %param.19) | copy-start | bytes 49156
  31.0 7.5 %copy-start.3 = (bf16[2,64,16,128]{3,2,1,0:T(8,128)(2,1)S(1)}, bf16[2,64,16,128]{3,2,1,0:T(8,128)(2,1)}, u32[]{:S(2)}) copy-start(bf16[2,64,16,128]{3,2,1,0:T(8,128)(2,1)} %get-tuple-element.18) | copy-start | bytes 1572868
  31.1 8.9 %copy-start.8 = (s32[2,8,3]{1,0,2:T(2,128)S(1)}, s32[2,8,3]{1,0,2:T(2,128)}, u32[]{:S(2)}) copy-start(s32[2,8,3]{1,0,2:T(2,128)} %param.12) | copy-start | bytes 580
  31.2 10.6 %copy-start.5 = (bf16[2,4,8,16,128]{4,3,2,1,0:T(8,128)(2,1)S(1)}, bf16[2,4,8,16,128]{4,3,2,1,0:T(8,128)(2,1)}, u32[]{:S(2)}) copy-start(bf16[2,4,8,16,128]{4,3,2,1,0:T(8,128)(2,1)} %get-tuple-element.17) | copy-start | bytes 786436
  32.5 33.2 %all-to-all-start = ((f16[32,132,128]{2,1,0:T(8,128)(2,1)}), f16[32,132,128]{2,1,0:T(8,128)(2,1)S(1)}, u32[]{:S(2)}, u32[]{:S(2)}) async-start(f16[32,132,128]{2,1,0:T(8,128)(2,1)} %pad_maximum_fusion.1), calls=%async_computation | async-start | bytes 2228224 | tf_op jit(solution)/shard_map/all_to_all | solution.py:311
  41.4 1.2 %copy-start.2 = (bf16[2,64,16,128]{1,3,2,0:T(8,128)(2,1)S(1)}, bf16[2,64,16,128]{1,3,2,0:T(8,128)(2,1)}, u32[]{:S(2)}) copy-start(bf16[2,64,16,128]{1,3,2,0:T(8,128)(2,1)} %copy.55) | copy-start | bytes 1572868
